TPU v7x, 256 devices: a whole 4x4x8 slice. The times are simulated.
256 devices in a mesh: pos: 32 (over x, y, core), freq: 8 (over z).
Axes of the slice: x: 4, y: 4, z: 8, core: 2. Of those that a mesh axis runs over, the one named last changes fastest.
Arguments:
- footprint: int32 [64, 32], replicated, may hold values from 0 to 1023, as said below
- basis: bfloat16 [64, 16, 2048, 256], P('pos', 'freq'), may hold values from -0.125 to 0.125
- weights: float32 [256], replicated, may hold values from 0.1 to 10
- conduct: float32 [2, 128, 256], P(None, 'pos', 'freq'), may hold values from 0.08 to 0.24
- baseline: float32 [128, 256], P('pos', 'freq'), may hold values from 0.2 to 2
Outputs:
- image: float32 [128, 256], P('pos', 'freq')
Inputs may be any that keep to these rules, and one draw needn't show every extreme that they name: `footprint`: tile t belongs to owner t // 32. Among the 64 entries of the rows of one index of pos, at most 4 lie in one owner's tiles, and in every draw one owner gets exactly 4 from every index of pos. Entries may repeat.
All inputs are finite; a program needn't handle non-finite values.
Results may differ from a plain program's by a relative error of at most 0.0003.
Values sent between devices are 32-bit elements; how exact they have to be, the bound alone decides.
A program may use at most 64 MiB of HBM per device.

v0:
```python
import math

import jax
import jax.numpy as jnp
from jax import lax
from jax.sharding import PartitionSpec as P

TH = 4
TW = 8
TILE_DEV = 32
PASSES = 3


elem_pitch = 0.125
cell_spacing = 0.7
top_depth = 4.0
eps_value = 1e-06


def padded(cells, sides, width):
    for axis, dim in sides:
        count = lax.axis_size(axis)
        ends = count - 1
        head = lax.slice_in_dim(cells, 0, width, axis=dim)
        tail = lax.slice_in_dim(cells, cells.shape[dim] - width, cells.shape[dim], axis=dim)
        cells = jnp.concatenate(
            [
                lax.ppermute(tail, axis, [(i, (i + 1) % count) for i in range(ends)]),
                cells,
                lax.ppermute(head, axis, [((i + 1) % count, i) for i in range(ends)]),
            ],
            axis=dim,
        )
    return cells


def green_rows(tile_ids, pos_global, freq_global, elements, positions, freqs):
    cells = jnp.arange(TH * TW)
    grid_row = (tile_ids // TILE_DEV)[:, None] * TH + (cells // TW)[None, :]
    grid_col = (tile_ids % TILE_DEV)[:, None] * TW + (cells % TW)[None, :]
    depth = top_depth + cell_spacing * grid_row.reshape(-1).astype(jnp.float32)
    lateral = cell_spacing * grid_col.reshape(-1).astype(jnp.float32)
    centre = pos_global.astype(jnp.float32) * (cell_spacing * TW * TILE_DEV / positions)
    element = (
        jnp.arange(elements).astype(jnp.float32) - 0.5 * (elements - 1)
    ) * elem_pitch + centre
    across = lateral[:, None] - element[None, :]
    distance = jnp.sqrt(depth[:, None] * depth[:, None] + across * across)
    wavenum = 2.0 * math.pi * (0.5 + freq_global.astype(jnp.float32) / freqs)
    amplitude = jnp.sqrt(top_depth / distance)
    phase = wavenum * distance
    return jnp.concatenate([amplitude * jnp.cos(phase), amplitude * jnp.sin(phase)], axis=1).astype(
        jnp.bfloat16
    )


def relax(values, across_k, along_k):
    centre_x = across_k[1:-1, 1:-1]
    centre_z = along_k[1:-1, 1:-1]
    middle = values[1:-1, 1:-1]
    north = jnp.minimum(centre_x, across_k[:-2, 1:-1]) * (values[:-2, 1:-1] - middle)
    south = jnp.minimum(centre_x, across_k[2:, 1:-1]) * (values[2:, 1:-1] - middle)
    west = jnp.minimum(centre_z, along_k[1:-1, :-2]) * (values[1:-1, :-2] - middle)
    east = jnp.minimum(centre_z, along_k[1:-1, 2:]) * (values[1:-1, 2:] - middle)
    return middle + north + south + west + east


def body(footprint, basis, weights, conduct, baseline):
    pos_local, freq_local, doubled, rank = basis.shape
    elements = doubled // 2
    foot_tiles = footprint.shape[1]
    pos_count = lax.axis_size("pos")
    freq_count = lax.axis_size("freq")
    positions = pos_local * pos_count
    freqs = freq_local * freq_count
    my_pos = lax.axis_index("pos")
    first_pos = my_pos * pos_local
    first_freq = lax.axis_index("freq") * freq_local
    tile_cells = TH * TW
    my_ids = lax.dynamic_slice_in_dim(footprint, first_pos, pos_local, 0)

    def one_position(inputs):
        tile_ids, local_basis, offset = inputs

        def add_freq(running, pair):
            freq_basis, freq_offset = pair
            green = green_rows(
                tile_ids, first_pos + offset, first_freq + freq_offset, elements, positions, freqs
            )
            return (running + jnp.dot(green, freq_basis, preferred_element_type=jnp.float32), None)

        start = jnp.zeros((foot_tiles * tile_cells, rank), jnp.float32)
        total, _ = lax.scan(add_freq, start, (local_basis, jnp.arange(freq_local)))
        return total

    partial_value = lax.map(one_position, (my_ids, basis, jnp.arange(pos_local)))
    rows = pos_local * foot_tiles
    partial_value = partial_value.reshape(rows, tile_cells, rank)
    capacity = max(2, 2 * rows // pos_count)
    slots = pos_count * capacity
    owners = my_ids.reshape(rows) // TILE_DEV
    owner_hot = (owners[:, None] == jnp.arange(pos_count)[None, :]).astype(jnp.int32)
    before = jnp.cumsum(owner_hot, axis=0) - owner_hot
    order_in = jnp.sum(before * owner_hot, axis=1)
    slot_of = owners * capacity + order_in
    placing = (jnp.arange(slots)[:, None] == slot_of[None, :]).astype(jnp.float32)
    all_ids = footprint.reshape(pos_count, rows)
    mine = (all_ids // TILE_DEV == my_pos).astype(jnp.int32)
    mine_rank = jnp.cumsum(mine, axis=1) - mine
    hitting = (mine[:, None, :] == 1) & (
        mine_rank[:, None, :] == jnp.arange(capacity)[None, :, None]
    )
    incoming = jnp.max(jnp.where(hitting, (all_ids % TILE_DEV)[:, None, :], -1), axis=2).reshape(
        slots
    )
    gathering = (jnp.arange(TILE_DEV)[:, None] == incoming[None, :]).astype(jnp.float32)
    local_tiles = TILE_DEV // freq_count
    packed = jnp.dot(
        placing,
        partial_value.reshape(rows, -1),
        precision=lax.Precision.HIGHEST,
        preferred_element_type=jnp.float32,
    )
    arrived = lax.all_to_all(
        packed.reshape(pos_count, capacity, -1), "pos", split_axis=0, concat_axis=0, tiled=True
    )
    compound = jnp.dot(
        gathering,
        arrived.reshape(slots, -1),
        precision=lax.Precision.HIGHEST,
        preferred_element_type=jnp.float32,
    ).reshape(TILE_DEV, tile_cells, rank)
    summed = lax.psum_scatter(compound, "freq", scatter_dimension=0, tiled=True)
    energy = jnp.sum(summed * summed * weights, axis=-1) / rank
    intensity = jnp.sqrt(energy + eps_value)
    field = intensity.reshape(local_tiles, TH, TW).transpose(1, 0, 2).reshape(TH, local_tiles * TW)
    field = field + baseline
    rims = padded(conduct, (("pos", 1), ("freq", 2)), 1)
    values = field
    for sweep in range(PASSES):
        widened = padded(values, (("pos", 0), ("freq", 1)), 1)
        values = relax(widened, rims[0], rims[1])
    return values


def solution(mesh):
    return jax.shard_map(
        body,
        mesh=mesh,
        in_specs=(P(), P("pos", "freq", None, None), P(), P(None, "pos", "freq"), P("pos", "freq")),
        out_specs=P("pos", "freq"),
        check_vma=False,
    )
```

profile of v0, /device:TPU:25, one launch (start us, length us, event | category | flops | bytes accessed | tf_op | source)
XLA Modules:
  0.0 295.8 jit_solution(7974694115496093014)
XLA Ops:
  8.9 97.2 %while.37 = (s32[]{:T(128)}, f32[2,1024,256]{2,1,0:T(8,128)}, bf16[2,2,2048,256]{3,2,1,0:T(8,128)(2,1)}, s32[2]{0:T(128)S(1)}, s32[2,32]{1,0:T(2,128)S(1)}, /*in...) while((s32[]{:T(128)}, f32[2,1024,256]{2,1,0:T(8,128)}, ...), condition=%wide.region_7.8_spmd, body=%wide.region_4.7_spmd.sunk | while | flops 1092105600 | bytes 17869636 | solution.py:96
  10.3 1.7 dynamic-slice_bitcast_fusion.2
  12.1 44.4 %while.38 = (s32[]{:T(128)}, f32[1024,256]{1,0:T(8,128)S(1)}, s32[32,1]{0,1:T(1,128)S(1)}, s32[32]{0:T(128)S(1)}, s32[32,1]{0,1:T(1,128)S(1)}, /*index=5*/s32[32...) while((s32[]{:T(128)}, f32[1024,256]{1,0:T(8,128)S(1)}, ...), condition=%wide.region_6.6_spmd.clone, body=%wide.region_5.5_spmd.clone.sunk | while | flops 1092105472 | bytes 11577071 | solution.py:93
  13.7 19.1 %multiply_convert_fusion.3 = (bf16[1024,1024]{1,0:T(8,128)(2,1)S(1)}, bf16[1024,1024]{1,0:T(8,128)(2,1)S(1)}) fusion(f32[]{:T(128)S(6)} %mul.288, f32[1024]{0:T(1024)S(1)} %multiply_add_fusion.7, f32[1024]{0:T(1024)S(1)} %mul.289, f32[1024]{0:T(1024)S(1)} %reshape.372), kind=kLoop, calls=%fused_computation.5.clone.1 | loop fusion | flops 9437184 | bytes 4206596 | tf_op jit(solution)/shard_map/convert
  32.9 1.4 fusion.48
  35.9 19.1 %multiply_convert_fusion.3 = (bf16[1024,1024]{1,0:T(8,128)(2,1)S(1)}, bf16[1024,1024]{1,0:T(8,128)(2,1)S(1)}) fusion(f32[]{:T(128)S(6)} %mul.288, f32[1024]{0:T(1024)S(1)} %multiply_add_fusion.7, f32[1024]{0:T(1024)S(1)} %mul.289, f32[1024]{0:T(1024)S(1)} %reshape.372), kind=kLoop, calls=%fused_computation.5.clone.1 | loop fusion | flops 9437184 | bytes 4206596 | tf_op jit(solution)/shard_map/convert
  55.0 1.4 fusion.48
  56.5 1.0 bitcast_dynamic-update-slice_fusion.2
  58.9 1.7 dynamic-slice_bitcast_fusion.2
  60.6 44.4 %while.38 = (s32[]{:T(128)}, f32[1024,256]{1,0:T(8,128)S(1)}, s32[32,1]{0,1:T(1,128)S(1)}, s32[32]{0:T(128)S(1)}, s32[32,1]{0,1:T(1,128)S(1)}, /*index=5*/s32[32...) while((s32[]{:T(128)}, f32[1024,256]{1,0:T(8,128)S(1)}, ...), condition=%wide.region_6.6_spmd.clone, body=%wide.region_5.5_spmd.clone.sunk | while | flops 1092105472 | bytes 11577071 | solution.py:93
  62.3 19.1 %multiply_convert_fusion.3 = (bf16[1024,1024]{1,0:T(8,128)(2,1)S(1)}, bf16[1024,1024]{1,0:T(8,128)(2,1)S(1)}) fusion(f32[]{:T(128)S(6)} %mul.288, f32[1024]{0:T(1024)S(1)} %multiply_add_fusion.7, f32[1024]{0:T(1024)S(1)} %mul.289, f32[1024]{0:T(1024)S(1)} %reshape.372), kind=kLoop, calls=%fused_computation.5.clone.1 | loop fusion | flops 9437184 | bytes 4206596 | tf_op jit(solution)/shard_map/convert
  81.4 1.4 fusion.48
  84.5 19.1 %multiply_convert_fusion.3 = (bf16[1024,1024]{1,0:T(8,128)(2,1)S(1)}, bf16[1024,1024]{1,0:T(8,128)(2,1)S(1)}) fusion(f32[]{:T(128)S(6)} %mul.288, f32[1024]{0:T(1024)S(1)} %multiply_add_fusion.7, f32[1024]{0:T(1024)S(1)} %mul.289, f32[1024]{0:T(1024)S(1)} %reshape.372), kind=kLoop, calls=%fused_computation.5.clone.1 | loop fusion | flops 9437184 | bytes 4206596 | tf_op jit(solution)/shard_map/convert
  103.6 1.4 fusion.48
  106.1 1.8 reshape.368
  107.9 1.9 fusion.17
  109.8 4.7 %copy.34 = f32[32,4,8192]{2,1,0:T(4,128)} copy(f32[32,4,8192]{2,0,1:T(8,128)S(1)} %fusion.17) | data formatting | bytes 8388608 | tf_op jit(solution)/shard_map/dot_general | solution.py:118
  114.5 7.8 %all-to-all-start = ((f32[32,4,8192]{2,1,0:T(4,128)}), f32[32,4,8192]{2,1,0:T(4,128)}, u32[]{:S(2)}, u32[]{:S(2)}) async-start(f32[32,4,8192]{2,1,0:T(4,128)} %copy.34), calls=%async_computation | async-start | bytes 8388608 | tf_op jit(solution)/shard_map/all_to_all | solution.py:124
  123.2 51.8 %all-to-all-done = f32[32,4,8192]{2,1,0:T(4,128)} async-done(((f32[32,4,8192]{2,1,0:T(4,128)}), f32[32,4,8192]{2,1,0:T(4,128)}, u32[]{:S(2)}, u32[]{:S(2)}) %all-to-all-start) | async-done | bytes 4194336 | tf_op jit(solution)/shard_map/all_to_all | solution.py:124
  175.1 5.4 %reshape.364 = f32[128,8192]{1,0:T(8,128)} reshape(f32[32,4,8192]{2,1,0:T(4,128)} %all-to-all-done) | data formatting | bytes 8388608 | tf_op jit(solution)/shard_map/reshape | solution.py:129
  180.5 5.6 %copy.35 = f32[8192,128]{1,0:T(8,128)} copy(f32[8192,128]{0,1:T(8,128)} %bitcast.60) | data formatting | bytes 8388608 | tf_op jit(solution)/shard_map/dot_general | solution.py:127
  186.0 4.6 %fusion.24 = f32[32,32,256]{2,0,1:T(8,128)S(1)} fusion(f32[32,256,128]{2,1,0:T(8,128)} %bitcast.59, s32[128]{0:T(128)S(1)} %eq.111), kind=kOutput, calls=%fused_computation.59 | convolution fusion | flops 402657280 | bytes 5243392 | tf_op jit(solution)/shard_map/dot_general | solution.py:127
  190.7 1.6 copy.36
  192.3 1.9 collective-permute-start
  194.3 2.4 collective-permute-start.1
  196.7 4.6 %collective-permute-done.1 = f32[2,1,32]{2,1,0:T(1,128)S(1)} collective-permute-done((f32[2,1,32]{2,1,0:T(1,128)S(1)}, f32[2,1,32]{2,1,0:T(1,128)S(1)}, u32[]{:S(2)}, u32[]{:S(2)}) %collective-permute-start.1) | collective-permute-done | bytes 288 | tf_op jit(solution)/shard_map/ppermute | solution.py:30
  201.3 3.5 %collective-permute-start.2 = (f32[2,6,1]{2,1,0:T(8,128)S(1)}, f32[2,6,1]{2,1,0:T(8,128)S(1)}, u32[]{:S(2)}, u32[]{:S(2)}) collective-permute-start(f32[2,6,1]{2,1,0:T(8,128)S(1)} %get-tuple-element.460), channel_id=1, source_target_pairs={{0,1},{1,2},{2,3},{3,4},{4,5},{5,6},{6,7},{8,9},{9,10},{10,11},{11... | collective-permute-start | bytes 152 | tf_op jit(solution)/shard_map/ppermute | solution.py:28
  204.9 1.3 collective-permute-start.3
  206.2 3.7 %collective-permute-done.3 = f32[2,6,1]{2,1,0:T(8,128)S(1)} collective-permute-done((f32[2,6,1]{2,1,0:T(8,128)S(1)}, f32[2,6,1]{2,1,0:T(8,128)S(1)}, u32[]{:S(2)}, u32[]{:S(2)}) %collective-permute-start.3) | collective-permute-done | bytes 80 | tf_op jit(solution)/shard_map/ppermute | solution.py:30
  209.9 17.9 %reduce-scatter.2.cloned.1.call-done = f32[4,32,256]{2,1,0:T(8,128)} async-done(((f32[32,32,256]{2,1,0:T(8,128)}), f32[4,32,256]{2,1,0:T(8,128)}) %reduce-scatter.2.cloned.1.call-update) | async-done | bytes 131088 | tf_op jit(solution)/shard_map/reduce_scatter | solution.py:133
  229.1 8.6 %collective-permute-start.4 = (f32[1,32]{1,0:T(1,128)S(1)}, f32[1,32]{1,0:T(1,128)S(1)}, u32[]{:S(2)}, u32[]{:S(2)}) collective-permute-start(f32[1,32]{1,0:T(1,128)S(1)} %get-tuple-element.486), channel_id=1, source_target_pairs={{0,8},{8,16},{16,24},{24,32},{32,40},{40,48},{48,56},{56,64},{64,7... | collective-permute-start | bytes 392 | tf_op jit(solution)/shard_map/ppermute | solution.py:28
  237.7 1.9 collective-permute-start.5
  239.6 5.0 %collective-permute-done.5 = f32[1,32]{1,0:T(1,128)S(1)} collective-permute-done((f32[1,32]{1,0:T(1,128)S(1)}, f32[1,32]{1,0:T(1,128)S(1)}, u32[]{:S(2)}, u32[]{:S(2)}) %collective-permute-start.5) | collective-permute-done | bytes 160 | tf_op jit(solution)/shard_map/ppermute | solution.py:30
  244.7 2.4 collective-permute-start.6
  247.1 1.3 collective-permute-start.7
  248.5 3.0 %collective-permute-done.7 = f32[6,1]{1,0:T(8,128)S(1)} collective-permute-done((f32[6,1]{1,0:T(8,128)S(1)}, f32[6,1]{1,0:T(8,128)S(1)}, u32[]{:S(2)}, u32[]{:S(2)}) %collective-permute-start.7) | collective-permute-done | bytes 56 | tf_op jit(solution)/shard_map/ppermute | solution.py:30
  251.7 3.4 %collective-permute-start.8 = (f32[1,32]{1,0:T(1,128)S(1)}, f32[1,32]{1,0:T(1,128)S(1)}, u32[]{:S(2)}, u32[]{:S(2)}) collective-permute-start(f32[1,32]{1,0:T(1,128)S(1)} %get-tuple-element.482), channel_id=1, source_target_pairs={{0,8},{8,16},{16,24},{24,32},{32,40},{40,48},{48,56},{56,64},{64,7... | collective-permute-start | bytes 392 | tf_op jit(solution)/shard_map/ppermute | solution.py:28
  255.1 1.9 collective-permute-start.9
  257.0 5.0 %collective-permute-done.9 = f32[1,32]{1,0:T(1,128)S(1)} collective-permute-done((f32[1,32]{1,0:T(1,128)S(1)}, f32[1,32]{1,0:T(1,128)S(1)}, u32[]{:S(2)}, u32[]{:S(2)}) %collective-permute-start.9) | collective-permute-done | bytes 160 | tf_op jit(solution)/shard_map/ppermute | solution.py:30
  262.1 2.8 collective-permute-start.10
  265.0 1.3 collective-permute-start.11
  266.3 3.3 %collective-permute-done.11 = f32[6,1]{1,0:T(8,128)S(1)} collective-permute-done((f32[6,1]{1,0:T(8,128)S(1)}, f32[6,1]{1,0:T(8,128)S(1)}, u32[]{:S(2)}, u32[]{:S(2)}) %collective-permute-start.11) | collective-permute-done | bytes 56 | tf_op jit(solution)/shard_map/ppermute | solution.py:30
  269.8 3.1 %collective-permute-start.12 = (f32[1,32]{1,0:T(1,128)S(1)}, f32[1,32]{1,0:T(1,128)S(1)}, u32[]{:S(2)}, u32[]{:S(2)}) collective-permute-start(f32[1,32]{1,0:T(1,128)S(1)} %get-tuple-element.478), channel_id=1, source_target_pairs={{0,8},{8,16},{16,24},{24,32},{32,40},{40,48},{48,56},{56,64},{64,7... | collective-permute-start | bytes 392 | tf_op jit(solution)/shard_map/ppermute | solution.py:28
  272.9 1.9 collective-permute-start.13
  274.8 5.0 %collective-permute-done.13 = f32[1,32]{1,0:T(1,128)S(1)} collective-permute-done((f32[1,32]{1,0:T(1,128)S(1)}, f32[1,32]{1,0:T(1,128)S(1)}, u32[]{:S(2)}, u32[]{:S(2)}) %collective-permute-start.13) | collective-permute-done | bytes 160 | tf_op jit(solution)/shard_map/ppermute | solution.py:30
  280.0 3.6 %collective-permute-start.14 = (f32[6,1]{1,0:T(8,128)S(1)}, f32[6,1]{1,0:T(8,128)S(1)}, u32[]{:S(2)}, u32[]{:S(2)}) collective-permute-start(f32[6,1]{1,0:T(8,128)S(1)} %get-tuple-element.462), channel_id=1, source_target_pairs={{0,1},{1,2},{2,3},{3,4},{4,5},{5,6},{6,7},{8,9},{9,10},{10,11},{11... | collective-permute-start | bytes 80 | tf_op jit(solution)/shard_map/ppermute | solution.py:28
  283.6 1.3 collective-permute-start.15
  284.9 3.3 %collective-permute-done.15 = f32[6,1]{1,0:T(8,128)S(1)} collective-permute-done((f32[6,1]{1,0:T(8,128)S(1)}, f32[6,1]{1,0:T(8,128)S(1)}, u32[]{:S(2)}, u32[]{:S(2)}) %collective-permute-start.15) | collective-permute-done | bytes 56 | tf_op jit(solution)/shard_map/ppermute | solution.py:30
  (115 shorter events, 12.0 us)
Async XLA Ops:
  7.9 1.0 copy-start
  106.1 1.8 copy-start.3
  106.1 1.8 copy-start.6
  114.5 8.0 %copy-start.1 = (s32[64,32]{1,0:T(8,128)S(1)}, s32[64,32]{1,0:T(8,128)}, u32[]{:S(2)}) copy-start(s32[64,32]{1,0:T(8,128)} %copy-done) | copy-start | bytes 24580
  114.5 60.6 %all-to-all-start = ((f32[32,4,8192]{2,1,0:T(4,128)}), f32[32,4,8192]{2,1,0:T(4,128)}, u32[]{:S(2)}, u32[]{:S(2)}) async-start(f32[32,4,8192]{2,1,0:T(4,128)} %copy.34), calls=%async_computation | async-start | bytes 8388608 | tf_op jit(solution)/shard_map/all_to_all | solution.py:124
  122.3 105.6 %reduce-scatter.2.cloned.1.call-start = ((), (), s32[]{:S(2)}) async-start(), calls=%async_computation.2 | async-start | bytes 1179648 | tf_op jit(solution)/shard_map/reduce_scatter | solution.py:133
  186.0 6.3 %copy-start.2 = (f32[2,4,32]{2,1,0:T(4,128)S(1)}, f32[2,4,32]{2,1,0:T(4,128)}, u32[]{:S(2)}) copy-start(f32[2,4,32]{2,1,0:T(4,128)} %param.12) | copy-start | bytes 3076
  186.0 41.8 %copy-start.5 = (f32[256]{0:T(256)S(1)}, f32[256]{0:T(256)}, u32[]{:S(2)}) copy-start(f32[256]{0:T(256)} %param.11) | copy-start | bytes 3076
  186.0 43.0 %copy-start.4 = (f32[4,32]{1,0:T(4,128)S(1)}, f32[4,32]{1,0:T(4,128)}, u32[]{:S(2)}) copy-start(f32[4,32]{1,0:T(4,128)} %param.13) | copy-start | bytes 1540
  192.3 4.3 %collective-permute-start = (f32[2,1,32]{2,1,0:T(1,128)S(1)}, f32[2,1,32]{2,1,0:T(1,128)S(1)}, u32[]{:S(2)}, u32[]{:S(2)}) collective-permute-start(f32[2,1,32]{2,1,0:T(1,128)S(1)} %get-tuple-element.466), channel_id=1, source_target_pairs={{0,8},{8,16},{16,24},{24,32},{32,40},{40,48},{48,56},{56,64},{64,7... | collective-permute-start | bytes 776 | tf_op jit(solution)/shard_map/ppermute | solution.py:28
  194.3 7.0 %collective-permute-start.1 = (f32[2,1,32]{2,1,0:T(1,128)S(1)}, f32[2,1,32]{2,1,0:T(1,128)S(1)}, u32[]{:S(2)}, u32[]{:S(2)}) collective-permute-start(f32[2,1,32]{2,1,0:T(1,128)S(1)} %get-tuple-element.467), channel_id=1, source_target_pairs={{8,0},{16,8},{24,16},{32,24},{40,32},{48,40},{56,48},{64,56},{72,6... | collective-permute-start | bytes 776 | tf_op jit(solution)/shard_map/ppermute | solution.py:30
  201.3 4.8 %collective-permute-start.2 = (f32[2,6,1]{2,1,0:T(8,128)S(1)}, f32[2,6,1]{2,1,0:T(8,128)S(1)}, u32[]{:S(2)}, u32[]{:S(2)}) collective-permute-start(f32[2,6,1]{2,1,0:T(8,128)S(1)} %get-tuple-element.460), channel_id=1, source_target_pairs={{0,1},{1,2},{2,3},{3,4},{4,5},{5,6},{6,7},{8,9},{9,10},{10,11},{11... | collective-permute-start | bytes 152 | tf_op jit(solution)/shard_map/ppermute | solution.py:28
  204.9 5.0 %collective-permute-start.3 = (f32[2,6,1]{2,1,0:T(8,128)S(1)}, f32[2,6,1]{2,1,0:T(8,128)S(1)}, u32[]{:S(2)}, u32[]{:S(2)}) collective-permute-start(f32[2,6,1]{2,1,0:T(8,128)S(1)} %get-tuple-element.461), channel_id=1, source_target_pairs={{1,0},{2,1},{3,2},{4,3},{5,4},{6,5},{7,6},{9,8},{10,9},{11,10},{12... | collective-permute-start | bytes 152 | tf_op jit(solution)/shard_map/ppermute | solution.py:30
  229.1 10.5 %collective-permute-start.4 = (f32[1,32]{1,0:T(1,128)S(1)}, f32[1,32]{1,0:T(1,128)S(1)}, u32[]{:S(2)}, u32[]{:S(2)}) collective-permute-start(f32[1,32]{1,0:T(1,128)S(1)} %get-tuple-element.486), channel_id=1, source_target_pairs={{0,8},{8,16},{16,24},{24,32},{32,40},{40,48},{48,56},{56,64},{64,7... | collective-permute-start | bytes 392 | tf_op jit(solution)/shard_map/ppermute | solution.py:28
  237.7 7.0 %collective-permute-start.5 = (f32[1,32]{1,0:T(1,128)S(1)}, f32[1,32]{1,0:T(1,128)S(1)}, u32[]{:S(2)}, u32[]{:S(2)}) collective-permute-start(f32[1,32]{1,0:T(1,128)S(1)} %get-tuple-element.487), channel_id=1, source_target_pairs={{8,0},{16,8},{24,16},{32,24},{40,32},{48,40},{56,48},{64,56},{72,6... | collective-permute-start | bytes 392 | tf_op jit(solution)/shard_map/ppermute | solution.py:30
  244.7 3.7 %collective-permute-start.6 = (f32[6,1]{1,0:T(8,128)S(1)}, f32[6,1]{1,0:T(8,128)S(1)}, u32[]{:S(2)}, u32[]{:S(2)}) collective-permute-start(f32[6,1]{1,0:T(8,128)S(1)} %get-tuple-element.468), channel_id=1, source_target_pairs={{0,1},{1,2},{2,3},{3,4},{4,5},{5,6},{6,7},{8,9},{9,10},{10,11},{11... | collective-permute-start | bytes 80 | tf_op jit(solution)/shard_map/ppermute | solution.py:28
  247.1 4.4 %collective-permute-start.7 = (f32[6,1]{1,0:T(8,128)S(1)}, f32[6,1]{1,0:T(8,128)S(1)}, u32[]{:S(2)}, u32[]{:S(2)}) collective-permute-start(f32[6,1]{1,0:T(8,128)S(1)} %get-tuple-element.469), channel_id=1, source_target_pairs={{1,0},{2,1},{3,2},{4,3},{5,4},{6,5},{7,6},{9,8},{10,9},{11,10},{12... | collective-permute-start | bytes 80 | tf_op jit(solution)/shard_map/ppermute | solution.py:30
  251.7 5.4 %collective-permute-start.8 = (f32[1,32]{1,0:T(1,128)S(1)}, f32[1,32]{1,0:T(1,128)S(1)}, u32[]{:S(2)}, u32[]{:S(2)}) collective-permute-start(f32[1,32]{1,0:T(1,128)S(1)} %get-tuple-element.482), channel_id=1, source_target_pairs={{0,8},{8,16},{16,24},{24,32},{32,40},{40,48},{48,56},{56,64},{64,7... | collective-permute-start | bytes 392 | tf_op jit(solution)/shard_map/ppermute | solution.py:28
  255.1 7.0 %collective-permute-start.9 = (f32[1,32]{1,0:T(1,128)S(1)}, f32[1,32]{1,0:T(1,128)S(1)}, u32[]{:S(2)}, u32[]{:S(2)}) collective-permute-start(f32[1,32]{1,0:T(1,128)S(1)} %get-tuple-element.483), channel_id=1, source_target_pairs={{8,0},{16,8},{24,16},{32,24},{40,32},{48,40},{56,48},{64,56},{72,6... | collective-permute-start | bytes 392 | tf_op jit(solution)/shard_map/ppermute | solution.py:30
  262.1 4.2 %collective-permute-start.10 = (f32[6,1]{1,0:T(8,128)S(1)}, f32[6,1]{1,0:T(8,128)S(1)}, u32[]{:S(2)}, u32[]{:S(2)}) collective-permute-start(f32[6,1]{1,0:T(8,128)S(1)} %get-tuple-element.464), channel_id=1, source_target_pairs={{0,1},{1,2},{2,3},{3,4},{4,5},{5,6},{6,7},{8,9},{9,10},{10,11},{11... | collective-permute-start | bytes 80 | tf_op jit(solution)/shard_map/ppermute | solution.py:28
  265.0 4.6 %collective-permute-start.11 = (f32[6,1]{1,0:T(8,128)S(1)}, f32[6,1]{1,0:T(8,128)S(1)}, u32[]{:S(2)}, u32[]{:S(2)}) collective-permute-start(f32[6,1]{1,0:T(8,128)S(1)} %get-tuple-element.465), channel_id=1, source_target_pairs={{1,0},{2,1},{3,2},{4,3},{5,4},{6,5},{7,6},{9,8},{10,9},{11,10},{12... | collective-permute-start | bytes 80 | tf_op jit(solution)/shard_map/ppermute | solution.py:30
  269.8 5.1 %collective-permute-start.12 = (f32[1,32]{1,0:T(1,128)S(1)}, f32[1,32]{1,0:T(1,128)S(1)}, u32[]{:S(2)}, u32[]{:S(2)}) collective-permute-start(f32[1,32]{1,0:T(1,128)S(1)} %get-tuple-element.478), channel_id=1, source_target_pairs={{0,8},{8,16},{16,24},{24,32},{32,40},{40,48},{48,56},{56,64},{64,7... | collective-permute-start | bytes 392 | tf_op jit(solution)/shard_map/ppermute | solution.py:28
  272.9 7.0 %collective-permute-start.13 = (f32[1,32]{1,0:T(1,128)S(1)}, f32[1,32]{1,0:T(1,128)S(1)}, u32[]{:S(2)}, u32[]{:S(2)}) collective-permute-start(f32[1,32]{1,0:T(1,128)S(1)} %get-tuple-element.479), channel_id=1, source_target_pairs={{8,0},{16,8},{24,16},{32,24},{40,32},{48,40},{56,48},{64,56},{72,6... | collective-permute-start | bytes 392 | tf_op jit(solution)/shard_map/ppermute | solution.py:30
  280.0 5.0 %collective-permute-start.14 = (f32[6,1]{1,0:T(8,128)S(1)}, f32[6,1]{1,0:T(8,128)S(1)}, u32[]{:S(2)}, u32[]{:S(2)}) collective-permute-start(f32[6,1]{1,0:T(8,128)S(1)} %get-tuple-element.462), channel_id=1, source_target_pairs={{0,1},{1,2},{2,3},{3,4},{4,5},{5,6},{6,7},{8,9},{9,10},{10,11},{11... | collective-permute-start | bytes 80 | tf_op jit(solution)/shard_map/ppermute | solution.py:28
  283.6 4.6 %collective-permute-start.15 = (f32[6,1]{1,0:T(8,128)S(1)}, f32[6,1]{1,0:T(8,128)S(1)}, u32[]{:S(2)}, u32[]{:S(2)}) collective-permute-start(f32[6,1]{1,0:T(8,128)S(1)} %get-tuple-element.463), channel_id=1, source_target_pairs={{1,0},{2,1},{3,2},{4,3},{5,4},{6,5},{7,6},{9,8},{10,9},{11,10},{12... | collective-permute-start | bytes 80 | tf_op jit(solution)/shard_map/ppermute | solution.py:30
Sparse Core Ops, SparseCore 0:
  192.4 35.4 reduce-scatter.1
where the time goes:
time: 297 us; the launch traced here: 296 us
  waiting for transfers between devices  103 us (35%)
  other arithmetic  81.1 us (27%)
  starting transfers between devices  50.8 us (17%)
  local copies, waits for them, and re-layouts  30.8 us (10%)
  between operations  13.8 us (5%)
  matrix products  12.1 us (4%)
  loops' own time  4.46 us (2%)
    another operation x4, other arithmetic  76.6 us
    all_to_all x1, waiting for transfers between devices, body(): lax.all_to_all(packed.reshape(pos_count, capacity, -1), 'pos', split_axis...  51.8 us
    ppermute x8, waiting for transfers between devices, padded(): lax.ppermute(head, axis, [((i + 1) % count, i) for i in range(ends)])  32.9 us
    ppermute x8, starting transfers between devices, padded(): lax.ppermute(tail, axis, [(i, (i + 1) % count) for i in range(ends)])  29.4 us
    reduce_scatter x1, waiting for transfers between devices, body(): summed = lax.psum_scatter(compound, 'freq', scatter_dimension=0, tiled=True)  17.9 us
    ppermute x8, starting transfers between devices, padded(): lax.ppermute(head, axis, [((i + 1) % count, i) for i in range(ends)])  13.3 us
    all_to_all x1, starting transfers between devices, body(): lax.all_to_all(packed.reshape(pos_count, capacity, -1), 'pos', split_axis...  7.81 us
    dot_general x2, local copies, waits for them, and re-layouts, body(): jnp.dot(gathering, arrived.reshape(slots, -1), precision=lax.Precision.HI...  7.16 us
  transfers between devices with their start and end apart: 18, of which 10 were waited for; matrix products, arithmetic and copies ran while one was open for 0% of the time, Pallas kernels for 0%

commit v1 on v0

v1 whole, which is shorter than its diff:
```python
import functools

import jax
import jax.numpy as jnp
from jax import lax
from jax.experimental import pallas as pl
from jax.experimental.pallas import tpu as pltpu
from jax.sharding import PartitionSpec as P

TH = 4
TW = 8
CELLS = TH * TW
TILE_DEV = 32
PASSES = 3
CAP = 4
EPS = 1e-06
MESH = pl.DeviceIdType.MESH

UNIT = 0.025
CELL = 28
PITCH = 5
TOP = 160
MAGIC = 12582912.0
SIN_POLY = (4.442879567546084, -7.307816684491789, 3.597774178087233, -0.7911993921613406)
COS_POLY = (
    1.4142134962552289,
    -6.978850948563853,
    5.7394603769076955,
    -1.8835579059892091,
    0.31068802753070307,
)
CHUNK = 256


def green_block(cross, depth_sq, turns):
    square = cross * cross + depth_sq
    dist = square * lax.rsqrt(square)
    amp = lax.rsqrt(dist) * ((TOP) ** 0.5)
    out = []
    for rate in turns:
        phase = dist * rate
        whole = (phase + MAGIC) - MAGIC
        part = phase - whole
        z = part * part
        s = ((SIN_POLY[3] * z + SIN_POLY[2]) * z + SIN_POLY[1]) * z + SIN_POLY[0]
        c = (((COS_POLY[4] * z + COS_POLY[3]) * z + COS_POLY[2]) * z + COS_POLY[1]) * z + COS_POLY[0]
        s = s * part
        q = amp * s
        out.append(((amp - q * s).astype(jnp.bfloat16), (q * c).astype(jnp.bfloat16)))
    return out


def make_unit(lat_ref, dep_ref, basis_v, green_s, rates, elements):
    rows = lat_ref.shape[1]
    chunks = elements // CHUNK

    def unit(col, p):
        total = None
        for kc in range(chunks):
            buf = green_s.at[kc % green_s.shape[0]]
            for lt in range(CHUNK // 128):
                start = PITCH * (kc * CHUNK + lt * 128)
                shift = (2 * CELL * col + (PITCH * (elements - 1) - 2 * start)).astype(jnp.float32) * 0.5
                for rg in range(rows // 16):
                    span = pl.ds(rg * 16, 16)
                    values = green_block(lat_ref[p, span, :] + shift, dep_ref[p, span, :], rates)
                    for f, (cosine, sine) in enumerate(values):
                        base = f * 2 * CHUNK + lt * 128
                        buf[span, pl.ds(base, 128)] = cosine
                        buf[span, pl.ds(base + CHUNK, 128)] = sine
            part = jnp.dot(buf[...], basis_v[p, kc], preferred_element_type=jnp.float32)
            total = part if total is None else total + part
        return total

    return unit


def split3(x):
    hi = x.astype(jnp.bfloat16)
    rest = x - hi.astype(jnp.float32)
    mid = rest.astype(jnp.bfloat16)
    low = (rest - mid.astype(jnp.float32)).astype(jnp.bfloat16)
    return hi, mid, low


def kernel(
    n_pos,
    n_freq,
    slot_ref,
    lat_ref,
    dep_ref,
    inc_ref,
    weight_ref,
    halo_ref,
    basis_ref,
    out_ref,
    basis_v,
    green_s,
    send_b,
    recv_b,
    final_b,
    packed,
    arrived,
    value_b,
    value_r,
    halo_r,
    basis_sem,
    ring_send,
    ring_recv,
    own_sem,
    a2a_send,
    a2a_recv,
    val_send,
    val_recv,
    halo_send,
    halo_recv,
):
    pos = lax.axis_index("pos")
    freq = lax.axis_index("freq")
    freq_local = basis_ref.shape[1]
    elements = basis_ref.shape[2] // 2
    freqs = freq_local * n_freq
    rows = lat_ref.shape[1]
    half = n_freq // 2
    messages = 4 * half - 2
    chunks = elements // CHUNK

    def other(dp, df):
        return (lax.rem(pos + dp + n_pos, n_pos), lax.rem(freq + df + n_freq, n_freq))

    barrier = pltpu.get_barrier_semaphore()
    near = [(dp, df) for dp in (-1, 0, 1) for df in range(n_freq) if (dp, df) != (0, 0)]
    sideways = [(dp, df) for dp, df in near if df != 0]
    for dp, df in sideways:
        pl.semaphore_signal(barrier, inc=1, device_id=other(dp, df), device_id_type=MESH)

    @pl.loop(1, n_pos)
    def _(step):
        pl.semaphore_signal(barrier, inc=1, device_id=other(step, 0), device_id_type=MESH)

    def basis_copies(p):
        copies = []
        for kc in range(chunks):
            for f in range(freq_local):
                for part in range(2):
                    copies.append(
                        pltpu.make_async_copy(
                            basis_ref.at[p, f, pl.ds(part * elements + kc * CHUNK, CHUNK), :],
                            basis_v.at[p, kc, pl.ds((2 * f + part) * CHUNK, CHUNK), :],
                            basis_sem.at[p, (kc * freq_local + f) * 2 + part],
                        )
                    )
        return copies

    first = basis_copies(0)
    second = basis_copies(1)
    for copy in first + second:
        copy.start()

    rates = [
        (freqs // 2 + freq * freq_local + f).astype(jnp.float32) * (UNIT / freqs)
        for f in range(freq_local)
    ]
    unit = make_unit(lat_ref, dep_ref, basis_v, green_s, rates, elements)

    def plan(u):
        way = 1 - 2 * lax.rem(u, 2)
        dist = half - (u + 2) // 4
        p = lax.rem((u + 1) // 2, 2)
        return way, lax.rem(freq + way * dist + n_freq, n_freq), p

    def ring_copy(u):
        way = 1 - 2 * lax.rem(u, 2)
        return pltpu.make_async_remote_copy(
            src_ref=send_b.at[u],
            dst_ref=recv_b.at[u],
            send_sem=ring_send.at[u],
            recv_sem=ring_recv.at[u],
            device_id=other(0, way),
            device_id_type=MESH,
        )

    for copy in first:
        copy.wait()
    for copy in second:
        copy.wait()

    @pl.loop(0, 2)
    def _(u):
        way, shard, p = plan(u)
        send_b[u] = unit(shard, p)

    pl.semaphore_wait(barrier, len(sideways) + n_pos - 1)

    ring_copy(0).start()
    ring_copy(1).start()

    halo_peers = [(dp, df) for dp in (-1, 0, 1) for df in (-1, 0, 1) if (dp, df) != (0, 0)]

    def halo_copy(i, dp, df):
        return pltpu.make_async_remote_copy(
            src_ref=halo_ref,
            dst_ref=halo_r.at[(1 - dp) * 3 + (1 - df)],
            send_sem=halo_send.at[i],
            recv_sem=halo_recv.at[(1 - dp) * 3 + (1 - df)],
            device_id=other(dp, df),
            device_id_type=MESH,
        )

    for i, (dp, df) in enumerate(halo_peers):
        halo_copy(i, dp, df).start()

    @pl.loop(2, messages + 2)
    def _(u):
        way, shard, p = plan(u)
        send_b[u] = unit(shard, p)

        @pl.when((u >= 4) & (u < messages))
        def _():
            ring_copy(u - 4).wait_recv()
            send_b[u] += recv_b[u - 4]

        @pl.when(u < messages)
        def _():
            ring_copy(u).start()

    for own, (right, left) in (
        (messages, (messages - 4, messages - 1)),
        (messages + 1, (messages - 2, messages - 3)),
    ):
        ring_copy(right).wait_recv()
        ring_copy(left).wait_recv()
        p = ((own + 1) // 2) % 2
        done = send_b[own] + recv_b[right] + recv_b[left]
        for e in range(rows // TH):
            final_b[p * (rows // TH) + e] = done[e * TH : (e + 1) * TH, :]

    for slot in range(n_pos * CAP):
        packed[slot] = final_b[slot_ref[slot]]

    def owner_copy(step):
        target = lax.rem(pos + step, n_pos)
        return pltpu.make_async_remote_copy(
            src_ref=packed.at[pl.ds(target * CAP, CAP)],
            dst_ref=arrived.at[pl.ds(pos * CAP, CAP)],
            send_sem=a2a_send.at[step],
            recv_sem=a2a_recv.at[step],
            device_id=(target, freq),
            device_id_type=MESH,
        )

    @pl.loop(1, n_pos)
    def _(step):
        owner_copy(step).start()

    mine = pl.ds(pos * CAP, CAP)
    own_copy = pltpu.make_async_copy(packed.at[mine], arrived.at[mine], own_sem)
    own_copy.start()

    cols = TILE_DEV * TW // n_freq
    for i, (dp, df) in enumerate(halo_peers):
        halo_copy(i, dp, df).wait_recv()
    lane16 = lax.broadcasted_iota(jnp.int32, (16, 128), 1)
    row16 = lax.broadcasted_iota(jnp.int32, (16, 128), 0)
    strips = []
    for dp in (-1, 0, 1):
        left = halo_r[(dp + 1) * 3]
        centre = halo_ref[...] if dp == 0 else halo_r[(dp + 1) * 3 + 1]
        right = halo_r[(dp + 1) * 3 + 2]
        strip = jnp.where(
            lane16 < PASSES,
            pltpu.roll(left, 128 - cols + PASSES, 1),
            jnp.where(
                lane16 < cols + PASSES,
                pltpu.roll(centre, PASSES, 1),
                pltpu.roll(right, cols + PASSES, 1),
            ),
        )
        strips.append(strip)
    grid_row = row16 + TH * (pos - 1)
    grid_col = lane16 + (cols * freq - PASSES)
    inside = (grid_row >= 0) & (grid_row < TH * n_pos) & (grid_col >= 0) & (grid_col < TILE_DEV * TW)
    inside = inside & (row16 < 3 * TH) & (lane16 < cols + 2 * PASSES)

    def widened(a):
        pieces = [strip[a * TH : (a + 1) * TH, :] for strip in strips]
        tall = jnp.concatenate(pieces + [pieces[0]], axis=0)
        return jnp.where(inside, tall, 0.0)

    across_k = widened(0)
    along_k = widened(1)
    ground = widened(2)
    south_k = jnp.minimum(across_k, pltpu.roll(across_k, 15, 0))
    north_k = jnp.minimum(across_k, pltpu.roll(across_k, 1, 0))
    east_k = jnp.minimum(along_k, pltpu.roll(along_k, 127, 1))
    west_k = jnp.minimum(along_k, pltpu.roll(along_k, 1, 1))

    slots = n_pos * CAP * TH
    place = (lax.broadcasted_iota(jnp.int32, (TH * TILE_DEV, slots), 0) == inc_ref[0:1, :]).astype(
        jnp.float32
    ).astype(jnp.bfloat16)

    @pl.loop(1, n_pos)
    def _(step):
        owner_copy(step).wait_recv()

    own_copy.wait()

    compound = None
    for piece in split3(arrived[...].reshape(slots, arrived.shape[2])):
        part = jnp.dot(place, piece, preferred_element_type=jnp.float32)
        compound = part if compound is None else compound + part
    rank = compound.shape[1]
    scaled = compound * compound * weight_ref[0:1, :]
    energy = lax.dot_general(
        jnp.ones((8, rank), jnp.float32),
        scaled,
        (((1,), (1,)), ((), ())),
        precision=lax.Precision.HIGHEST,
        preferred_element_type=jnp.float32,
    )
    value_b[...] = jnp.sqrt(energy / rank + EPS)

    def value_copy(i, dp, df):
        return pltpu.make_async_remote_copy(
            src_ref=value_b,
            dst_ref=value_r.at[(1 - dp) * n_freq + freq],
            send_sem=val_send.at[i],
            recv_sem=val_recv.at[i],
            device_id=other(dp, df),
            device_id_type=MESH,
        )

    for i, (dp, df) in enumerate(near):
        value_copy(i, dp, df).start()

    value_r[n_freq + freq] = value_b[...]

    from_r = lax.broadcasted_iota(jnp.int32, (128, TH * 128), 0)
    to_n = lax.broadcasted_iota(jnp.int32, (128, TH * 128), 1)
    to_col = to_n % 128 + (cols * freq - PASSES) + TW
    chosen = (from_r // TILE_DEV == to_n // 128) & (from_r % TILE_DEV == to_col // TW - 1)
    spread = chosen.astype(jnp.float32).astype(jnp.bfloat16)
    sub24 = lax.broadcasted_iota(jnp.int32, (3 * TW, TH * 128), 0)
    col24 = lax.broadcasted_iota(jnp.int32, (3 * TW, TH * 128), 1)
    keep = (col24 % 128 + (cols * freq - PASSES) + TW) % TW == sub24 % TW
    sub8 = lax.broadcasted_iota(jnp.int32, (TW, 128), 0)

    for i, (dp, df) in enumerate(near):
        value_copy(i, dp, df).wait_recv()

    groups = []
    for o in range(3):
        group = value_r[o * n_freq]
        for col in range(1, n_freq):
            group = jnp.where(sub8 == col, value_r[o * n_freq + col], group)
        groups.append(group)
    stacked = jnp.concatenate(groups, axis=0)
    wide = None
    for piece in split3(stacked):
        part = jnp.dot(piece, spread, preferred_element_type=jnp.float32)
        wide = part if wide is None else wide + part
    wide = jnp.where(keep, wide, 0.0)
    field = jnp.zeros((16, 128), jnp.float32)
    for o in range(3):
        summed = jnp.sum(wide[o * TW : (o + 1) * TW, :], axis=0, keepdims=True)
        for r in range(TH):
            field = jnp.where(row16 == o * TH + r, summed[:, r * 128 : (r + 1) * 128], field)
    u = jnp.where(inside, field + ground, 0.0)
    for sweep in range(PASSES):
        north = north_k * (pltpu.roll(u, 1, 0) - u)
        south = south_k * (pltpu.roll(u, 15, 0) - u)
        west = west_k * (pltpu.roll(u, 1, 1) - u)
        east = east_k * (pltpu.roll(u, 127, 1) - u)
        u = u + north + south + west + east
    u = pltpu.roll(u, 128 - PASSES, 1)
    out_ref[...] = u[TH : 2 * TH, :cols]

    @pl.loop(0, messages)
    def _(u):
        ring_copy(u).wait_send()

    @pl.loop(1, n_pos)
    def _(step):
        owner_copy(step).wait_send()

    for i, (dp, df) in enumerate(halo_peers):
        halo_copy(i, dp, df).wait_send()
    for i, (dp, df) in enumerate(near):
        value_copy(i, dp, df).wait_send()


def body(footprint, basis, weights, conduct, baseline):
    pos_local, freq_local, doubled, rank = basis.shape
    elements = doubled // 2
    foot = footprint.shape[1]
    n_pos = lax.axis_size("pos")
    n_freq = lax.axis_size("freq")
    positions = pos_local * n_pos
    my_pos = lax.axis_index("pos")
    rows = foot * TH
    entries = pos_local * foot
    blocks = footprint.reshape(n_pos, entries)
    my_ids = lax.dynamic_slice_in_dim(footprint, my_pos * pos_local, pos_local, 0)

    depth = TOP + CELL * ((my_ids // TILE_DEV)[:, :, None] * TH + jnp.arange(TH)[None, None, :])
    centre = (my_pos * pos_local + jnp.arange(pos_local)) * (CELL * TW * TILE_DEV // positions)
    lateral = CELL * TW * (my_ids % TILE_DEV) - centre[:, None]
    lateral = jnp.broadcast_to(lateral[:, :, None], depth.shape).reshape(pos_local, rows, 1)
    lat = (lateral - PITCH * jnp.arange(128)[None, None, :]).astype(jnp.float32)
    depth = depth.reshape(pos_local, rows, 1).astype(jnp.float32)
    dep = jnp.broadcast_to(depth * depth, lat.shape)

    flat = my_ids.reshape(entries)
    owner = flat // TILE_DEV
    earlier = jnp.arange(entries)[None, :] < jnp.arange(entries)[:, None]
    order = jnp.sum(((owner[:, None] == owner[None, :]) & earlier).astype(jnp.int32), axis=1)
    slot_of = owner * CAP + order
    slots = jnp.arange(n_pos * CAP)
    slot = jnp.sum(
        jnp.where(slots[:, None] == slot_of[None, :], jnp.arange(entries)[None, :], 0), axis=1
    ).astype(jnp.int32)
    mine = blocks // TILE_DEV == my_pos
    rank_in = jnp.dot(
        mine.astype(jnp.bfloat16),
        earlier.T.astype(jnp.bfloat16),
        preferred_element_type=jnp.float32,
    ).astype(jnp.int32)
    hit = mine[:, None, :] & (rank_in[:, None, :] == jnp.arange(CAP)[None, :, None])
    tile = jnp.max(jnp.where(hit, (blocks % TILE_DEV)[:, None, :], -1), axis=2)
    inc = jnp.where(
        tile[:, :, None] >= 0, tile[:, :, None] + TILE_DEV * jnp.arange(TH)[None, None, :], -1
    ).reshape(1, n_pos * CAP * TH)

    cols = baseline.shape[1]
    halo = jnp.concatenate([conduct.reshape(2 * TH, cols), baseline], axis=0)
    halo = jnp.pad(halo, ((0, 4), (0, 128 - cols)))

    messages = 2 * n_freq - 2
    near = 3 * n_freq - 1
    vmem = pl.BlockSpec(memory_space=pltpu.VMEM)
    return pl.pallas_call(
        functools.partial(kernel, n_pos, n_freq),
        out_shape=jax.ShapeDtypeStruct(baseline.shape, jnp.float32),
        in_specs=[pl.BlockSpec(memory_space=pltpu.SMEM)]
        + [vmem] * 5
        + [pl.BlockSpec(memory_space=pltpu.MemorySpace.HBM)],
        out_specs=vmem,
        scratch_shapes=[
            pltpu.VMEM((pos_local, elements // CHUNK, 2 * freq_local * CHUNK, rank), jnp.bfloat16),
            pltpu.VMEM((elements // CHUNK, rows, 2 * freq_local * CHUNK), jnp.bfloat16),
            pltpu.VMEM((messages + 2, rows, rank), jnp.float32),
            pltpu.VMEM((messages, rows, rank), jnp.float32),
            pltpu.VMEM((entries, TH, rank), jnp.float32),
            pltpu.VMEM((n_pos * CAP, TH, rank), jnp.float32),
            pltpu.VMEM((n_pos * CAP, TH, rank), jnp.float32),
            pltpu.VMEM((8, 128), jnp.float32),
            pltpu.VMEM((3 * n_freq, 8, 128), jnp.float32),
            pltpu.VMEM((9, 16, 128), jnp.float32),
            pltpu.SemaphoreType.DMA((pos_local, elements // CHUNK * freq_local * 2)),
            pltpu.SemaphoreType.DMA((messages,)),
            pltpu.SemaphoreType.DMA((messages,)),
            pltpu.SemaphoreType.DMA,
            pltpu.SemaphoreType.DMA((n_pos,)),
            pltpu.SemaphoreType.DMA((n_pos,)),
            pltpu.SemaphoreType.DMA((near,)),
            pltpu.SemaphoreType.DMA((near,)),
            pltpu.SemaphoreType.DMA((8,)),
            pltpu.SemaphoreType.DMA((9,)),
        ],
        compiler_params=pltpu.CompilerParams(
            collective_id=0, has_side_effects=True, vmem_limit_bytes=48 * 1024 * 1024
        ),
    )(slot, lat, dep, inc, weights.reshape(1, rank), halo, basis)


def solution(mesh):
    return jax.shard_map(
        body,
        mesh=mesh,
        in_specs=(P(), P("pos", "freq", None, None), P(), P(None, "pos", "freq"), P("pos", "freq")),
        out_specs=P("pos", "freq"),
        check_vma=False,
    )
```

time: 297 us -> 63.8 us (0.21)
  the two profiles are of different devices: /device:TPU:25 before, /device:TPU:1 now
where the time goes in v1:
time: 63.8 us; the launch traced here: 63.5 us
  Pallas kernels  56.5 us (89%)
  local copies, waits for them, and re-layouts  5.27 us (8%)
  other arithmetic  1.54 us (2%)
    pallas_call x1, Pallas kernels, body(): pl.pallas_call(functools.partial(kernel, n_pos, n_freq), out_shape=jax.Sh...  56.5 us
    unnamed x6, local copies, waits for them, and re-layouts  4.25 us

profile of v1, /device:TPU:1, one launch (start us, length us, event | category | flops | bytes accessed | tf_op | source)
XLA Modules:
  0.0 63.5 jit_solution(5880386005382409729)
XLA Ops:
  0.0 0.7 %select_maximum_fusion.halo_ref = f32[16,128]{1,0:T(8,128)S(1)} fusion(f32[4,32]{1,0:T(4,128)} %param.9, f32[8,32]{1,0:T(8,128)} %bitcast.4), kind=kLoop, calls=%fused_computation.20 | loop fusion | flops 16384 | bytes 9728 | tf_op jit(solution)/shard_map/concatenate | solution.py:436
  0.7 0.1 add.120
  0.8 0.8 %copy.19 = s32[64,32]{1,0:T(8,128)S(1)} copy(s32[64,32]{0,1:T(8,128)} %param.5) | data formatting | bytes 16384 | tf_op args[0]
  1.7 0.1 reshape.223
  1.7 0.1 reshape.222
  1.8 0.1 fusion.6
  1.9 0.2 convert_reduce_fusion
  2.1 0.1 select_reduce_fusion.1.slot_ref
  2.2 0.1 convolution_convert_fusion
  2.4 0.2 select_reduce_fusion
  2.5 0.1 copy.21
  2.6 0.1 copy.22
  2.7 0.1 broadcast_in_dim.38
  2.8 0.1 sub.44
  2.9 0.1 add.117
  3.0 0.1 add.118
  3.1 0.1 add_select_fusion
  3.3 0.1 select_n.81.inc_ref
  3.4 0.1 subtract_convert_fusion.lat_ref
  3.5 0.1 broadcast_in_dim.39.dep_ref
  3.6 0.0 copy-start
  3.6 2.2 %copy-done = bf16[2,2,2048,256]{3,2,1,0:T(8,128)(2,1)S(1)} copy-done((bf16[2,2,2048,256]{3,2,1,0:T(8,128)(2,1)S(1)}, bf16[2,2,2048,256]{3,2,1,0:T(8,128)(2,1)}, u32[]{:S(2)}) %copy-start) | copy-done | bytes 4194328
  5.8 0.0 copy-start.1
  5.8 0.7 %copy-done.1 = f32[256]{0:T(256)S(1)} copy-done((f32[256]{0:T(256)S(1)}, f32[256]{0:T(256)}, u32[]{:S(2)}) %copy-start.1) | copy-done | bytes 1048
  6.5 56.5 %shard_map.55 = f32[4,32]{1,0:T(4,128)S(1)} custom-call(s32[128]{0:T(128)S(1)} %select_reduce_fusion.1.slot_ref, f32[2,128,128]{2,1,0:T(8,128)S(1)} %subtract_convert_fusion.lat_ref, f32[2,128,128]{2,1,0:T(8,128)S(1)} %broadcast_in_dim.39.dep_ref, s32[1,512]{1,0:T(1,128)S(1)} %select_n.81.inc_ref, f32[1,256]{1,0:T(1,128)S(1)} %bitcast.3, ...), custom_call_target="tpu_custom_call" | custom-call | tf_op jit(solution)/shard_map/pallas_call | solution.py:442
  63.0 0.6 copy.24
  (11 shorter events, 0.1 us)
Async XLA Ops:
  3.6 2.2 %copy-start = (bf16[2,2,2048,256]{3,2,1,0:T(8,128)(2,1)S(1)}, bf16[2,2,2048,256]{3,2,1,0:T(8,128)(2,1)}, u32[]{:S(2)}) copy-start(bf16[2,2,2048,256]{3,2,1,0:T(8,128)(2,1)} %basis_ref.1) | copy-start | bytes 12582916
  5.8 0.7 %copy-start.1 = (f32[256]{0:T(256)S(1)}, f32[256]{0:T(256)}, u32[]{:S(2)}) copy-start(f32[256]{0:T(256)} %param.7) | copy-start | bytes 3076

commit v2 on v1

v2 whole, which is shorter than its diff:
```python
import functools

import jax
import jax.numpy as jnp
from jax import lax
from jax.experimental import pallas as pl
from jax.experimental.pallas import tpu as pltpu
from jax.sharding import PartitionSpec as P

TH = 4
TW = 8
CELLS = TH * TW
TILE_DEV = 32
PASSES = 3
CAP = 4
EPS = 1e-06
MESH = pl.DeviceIdType.MESH

UNIT = 0.025
CELL = 28
PITCH = 5
TOP = 160
SIN_POLY = (-4.547240826688576, 9.23637803174852, -5.615372827081364)
SCALE_SQ = 0.6259964781564749
DOUBLE = (2.0 + 1e-6) / SCALE_SQ
LANES = 128


def green_block(cross, depth_sq, turns):
    square = cross * cross + depth_sq
    dist = square * lax.rsqrt(square)
    root = lax.rsqrt(dist)
    amp = root * (TOP**0.5)
    scaled_amp = root * (TOP**0.5 * SCALE_SQ)
    out = []
    for rate in turns:
        phase = dist * rate
        x = jnp.round(phase) - phase
        z = x * x
        s = x * (((z + SIN_POLY[0]) * z + SIN_POLY[1]) * z + SIN_POLY[2])
        w = DOUBLE - s * s
        u = w * scaled_amp
        out.append(((u - amp).astype(jnp.bfloat16), (u * s * lax.rsqrt(w)).astype(jnp.bfloat16)))
    return out


def make_unit(lat_ref, dep_ref, basis_v, green_s, rates, elements):
    rows = lat_ref.shape[1]

    def unit(col, p):
        total = None
        for tile in range(elements // LANES):
            start = tile * LANES
            shift = (2 * CELL * col + (PITCH * (elements - 1) - 2 * PITCH * start)).astype(jnp.float32) * 0.5
            for rg in range(rows // 16):
                span = pl.ds(rg * 16, 16)
                values = green_block(lat_ref[p, span, :] + shift, dep_ref[p, span, :], rates)
                for f, (cosine, sine) in enumerate(values):
                    green_s[tile, f, span, 0:LANES] = cosine
                    green_s[tile, f, span, LANES : 2 * LANES] = sine
            for f in range(len(rates)):
                right = jnp.concatenate(
                    [
                        basis_v[p, f, start : start + LANES, :],
                        basis_v[p, f, elements + start : elements + start + LANES, :],
                    ],
                    axis=0,
                )
                part = jnp.dot(green_s[tile, f], right, preferred_element_type=jnp.float32)
                total = part if total is None else total + part
        return total

    return unit


def split3(x):
    hi = x.astype(jnp.bfloat16)
    rest = x - hi.astype(jnp.float32)
    mid = rest.astype(jnp.bfloat16)
    low = (rest - mid.astype(jnp.float32)).astype(jnp.bfloat16)
    return hi, mid, low


def kernel(
    n_pos,
    n_freq,
    foot_ref,
    weight_ref,
    conduct_ref,
    base_ref,
    basis_ref,
    out_ref,
    foot_v,
    weight_v,
    conduct_v,
    base_v,
    lat_v,
    dep_v,
    basis_v,
    green_s,
    send_b,
    recv_b,
    final_b,
    packed,
    arrived,
    value_b,
    value_r,
    halo_b,
    halo_r,
    slot_v,
    slot_s,
    in_sem,
    basis_sem,
    ring_send,
    ring_recv,
    own_sem,
    a2a_send,
    a2a_recv,
    val_send,
    val_recv,
    halo_send,
    halo_recv,
):
    pos = lax.axis_index("pos")
    freq = lax.axis_index("freq")
    pos_local, freq_local, doubled, rank = basis_ref.shape
    elements = doubled // 2
    freqs = freq_local * n_freq
    foot = foot_v.shape[0]
    rows = foot * TH
    entries = pos_local * foot
    half = n_freq // 2
    messages = 4 * half - 2
    iota = lax.broadcasted_iota

    loads = [
        pltpu.make_async_copy(src, dst, in_sem.at[i])
        for i, (src, dst) in enumerate(
            ((foot_ref, foot_v), (conduct_ref, conduct_v), (base_ref, base_v), (weight_ref, weight_v))
        )
    ]
    basis_loads = [
        pltpu.make_async_copy(basis_ref.at[p], basis_v.at[p], basis_sem.at[p]) for p in range(pos_local)
    ]
    loads[0].start()
    for copy in basis_loads:
        copy.start()
    for copy in loads[1:]:
        copy.start()

    def other(dp, df):
        return (lax.rem(pos + dp + n_pos, n_pos), lax.rem(freq + df + n_freq, n_freq))

    barrier = pltpu.get_barrier_semaphore()
    near = [(dp, df) for dp in (-1, 0, 1) for df in range(n_freq) if (dp, df) != (0, 0)]
    sideways = [(dp, df) for dp, df in near if df != 0]

    @pl.loop(1, n_pos)
    def _(step):
        pl.semaphore_signal(barrier, inc=1, device_id=other(step, 0), device_id_type=MESH)

    for dp, df in sideways:
        pl.semaphore_signal(barrier, inc=1, device_id=other(dp, df), device_id_type=MESH)

    loads[0].wait()
    positions = pos_local * n_pos
    expand = iota(jnp.int32, (rows, foot), 0) // TH == iota(jnp.int32, (rows, foot), 1)
    expand = jnp.where(expand, 1.0, 0.0).astype(jnp.bfloat16)
    foot_all = foot_v[...]
    owner_of = jnp.dot(
        expand,
        (foot_all // TILE_DEV).astype(jnp.float32).astype(jnp.bfloat16),
        preferred_element_type=jnp.float32,
    )
    local_of = jnp.dot(
        expand,
        (foot_all % TILE_DEV).astype(jnp.float32).astype(jnp.bfloat16),
        preferred_element_type=jnp.float32,
    )
    corner = iota(jnp.int32, (rows, 1), 0) % TH
    which = iota(jnp.int32, (rows, positions), 1)
    for p in range(pos_local):
        position = pos * pos_local + p
        owner = jnp.sum(jnp.where(which == position, owner_of, 0.0), axis=1, keepdims=True)
        local = jnp.sum(jnp.where(which == position, local_of, 0.0), axis=1, keepdims=True)
        depth = (TOP + CELL * (owner.astype(jnp.int32) * TH + corner)).astype(jnp.float32)
        centre = position * (CELL * TW * TILE_DEV // positions)
        lateral = CELL * TW * local.astype(jnp.int32) - centre
        lat_v[p] = (lateral - PITCH * iota(jnp.int32, (rows, LANES), 1)).astype(jnp.float32)
        dep_v[p] = jnp.broadcast_to(depth * depth, (rows, LANES))

    rates = [
        (freqs // 2 + freq * freq_local + f).astype(jnp.float32) * (UNIT / freqs)
        for f in range(freq_local)
    ]
    unit = make_unit(lat_v, dep_v, basis_v, green_s, rates, elements)

    def plan(u):
        way = 1 - 2 * lax.rem(u, 2)
        dist = half - (u + 2) // 4
        p = lax.rem((u + 1) // 2, 2)
        return way, lax.rem(freq + way * dist + n_freq, n_freq), p

    def compute(u):
        way, shard, p = plan(u)
        done = unit(shard, p)
        for h in range(2):
            send_b[u, h] = done[:, h * LANES : (h + 1) * LANES]

    def ring_copy(u):
        return pltpu.make_async_remote_copy(
            src_ref=send_b.at[u],
            dst_ref=recv_b.at[u],
            send_sem=ring_send.at[u, 0],
            recv_sem=ring_recv.at[u, 0],
            device_id=other(0, 1 - 2 * lax.rem(u, 2)),
            device_id_type=MESH,
        )

    def ring_half(u, h):
        return pltpu.make_async_remote_copy(
            src_ref=send_b.at[u, h],
            dst_ref=recv_b.at[u, h],
            send_sem=ring_send.at[u, h],
            recv_sem=ring_recv.at[u, h],
            device_id=other(0, 1 - 2 * lax.rem(u, 2)),
            device_id_type=MESH,
        )

    @pl.loop(0, 2)
    def _(u):
        @pl.when(u == 0)
        def _():
            basis_loads[0].wait()

        @pl.when(u == 1)
        def _():
            basis_loads[1].wait()

        compute(u)

    for copy in loads[1:]:
        copy.wait()
    cols = base_v.shape[1]
    halo_b[...] = jnp.zeros(halo_b.shape, jnp.float32)
    halo_b[0:TH, 0:cols] = conduct_v[0]
    halo_b[TH : 2 * TH, 0:cols] = conduct_v[1]
    halo_b[2 * TH : 3 * TH, 0:cols] = base_v[...]

    pl.semaphore_wait(barrier, len(sideways) + n_pos - 1)

    ring_copy(0).start()
    ring_copy(1).start()

    halo_peers = [(dp, df) for dp in (-1, 0, 1) for df in (-1, 0, 1) if (dp, df) != (0, 0)]

    def halo_copy(i, dp, df):
        return pltpu.make_async_remote_copy(
            src_ref=halo_b,
            dst_ref=halo_r.at[(1 - dp) * 3 + (1 - df)],
            send_sem=halo_send.at[i],
            recv_sem=halo_recv.at[(1 - dp) * 3 + (1 - df)],
            device_id=other(dp, df),
            device_id_type=MESH,
        )

    @pl.loop(2, messages + 2)
    def _(u):
        compute(u)

        @pl.when((u >= 4) & (u < messages))
        def _():
            ring_copy(u - 4).wait_recv()
            send_b[u] += recv_b[u - 4]

        @pl.when(u < messages - 4)
        def _():
            ring_copy(u).start()

        @pl.when((u >= messages - 4) & (u < messages))
        def _():
            ring_half(u, 0).start()

        @pl.when(u == messages - 1)
        def _():
            for back in range(4):
                ring_half(messages - 4 + back, 1).start()

        @pl.when(u == 2)
        def _():
            for i, (dp, df) in enumerate(halo_peers):
                halo_copy(i, dp, df).start()

    foot_f = foot_all.astype(jnp.float32)
    which = iota(jnp.int32, (foot, positions), 1)
    flat_col = jnp.concatenate(
        [
            jnp.sum(jnp.where(which == pos * pos_local + p, foot_f, 0.0), axis=1, keepdims=True)
            for p in range(pos_local)
        ],
        axis=0,
    )
    to_self = iota(jnp.int32, (entries, entries), 0) == iota(jnp.int32, (entries, entries), 1)
    flat_row = jnp.sum(jnp.where(to_self, flat_col, 0.0), axis=0, keepdims=True)
    owner_row = flat_row.astype(jnp.int32) // TILE_DEV
    owner_col = flat_col.astype(jnp.int32) // TILE_DEV
    earlier = iota(jnp.int32, (entries, entries), 1) < iota(jnp.int32, (entries, entries), 0)
    order = jnp.sum(
        jnp.where((owner_row == owner_col) & earlier, 1.0, 0.0), axis=1, keepdims=True
    ).astype(jnp.int32)
    slot_of = owner_col * CAP + order
    all_slots = n_pos * CAP
    here = slot_of == iota(jnp.int32, (entries, all_slots), 1)
    entry = iota(jnp.int32, (entries, all_slots), 0).astype(jnp.float32)
    slot_v[...] = jnp.sum(jnp.where(here, entry, 0.0), axis=0, keepdims=True).astype(jnp.int32)
    slot_load = pltpu.make_async_copy(slot_v, slot_s, own_sem.at[2])
    slot_load.start()

    spans = n_pos * CAP * TH
    mine = foot_all // TILE_DEV == pos
    mine_b = jnp.where(mine, 1.0, 0.0).astype(jnp.bfloat16)
    lower = iota(jnp.int32, (foot, foot), 1) < iota(jnp.int32, (foot, foot), 0)
    from_p = iota(jnp.int32, (positions, positions), 0)
    to_p = iota(jnp.int32, (positions, positions), 1)
    later = (from_p // pos_local == to_p // pos_local) & (from_p < to_p)
    moved = jnp.dot(
        mine_b, jnp.where(later, 1.0, 0.0).astype(jnp.bfloat16), preferred_element_type=jnp.float32
    )
    ahead = jnp.dot(
        jnp.where(lower, 1.0, 0.0).astype(jnp.bfloat16), mine_b, preferred_element_type=jnp.float32
    ) + jnp.sum(moved, axis=0, keepdims=True)
    local = (foot_all % TILE_DEV + 1).astype(jnp.float32)
    found = jnp.concatenate(
        [
            jnp.sum(jnp.where(mine & (ahead == s), local, 0.0), axis=0, keepdims=True)
            for s in range(CAP)
        ],
        axis=0,
    )
    block_of = iota(jnp.int32, (positions, spans), 0) // pos_local
    block_to = iota(jnp.int32, (positions, spans), 1) // (TH * CAP)
    table = jnp.dot(
        found.astype(jnp.bfloat16),
        jnp.where(block_of == block_to, 1.0, 0.0).astype(jnp.bfloat16),
        preferred_element_type=jnp.float32,
    )
    turn = iota(jnp.int32, (CAP, spans), 1) // TH % CAP == iota(jnp.int32, (CAP, spans), 0)
    tile_in = jnp.sum(jnp.where(turn, table, 0.0), axis=0, keepdims=True).astype(jnp.int32)
    corner_in = iota(jnp.int32, (1, spans), 1) % TH
    target_row = jnp.where(tile_in > 0, tile_in - 1 + TILE_DEV * corner_in, -1)
    place = jnp.where(iota(jnp.int32, (TH * TILE_DEV, spans), 0) == target_row, 1.0, 0.0)
    place = place.astype(jnp.bfloat16)

    for i, (dp, df) in enumerate(halo_peers):
        halo_copy(i, dp, df).wait_recv()
    lane16 = iota(jnp.int32, (16, LANES), 1)
    row16 = iota(jnp.int32, (16, LANES), 0)
    strips = []
    for dp in (-1, 0, 1):
        left = halo_r[(dp + 1) * 3]
        centre = halo_b[...] if dp == 0 else halo_r[(dp + 1) * 3 + 1]
        right = halo_r[(dp + 1) * 3 + 2]
        strip = jnp.where(
            lane16 < PASSES,
            pltpu.roll(left, LANES - cols + PASSES, 1),
            jnp.where(
                lane16 < cols + PASSES,
                pltpu.roll(centre, PASSES, 1),
                pltpu.roll(right, cols + PASSES, 1),
            ),
        )
        strips.append(strip)
    grid_row = row16 + TH * (pos - 1)
    grid_col = lane16 + (cols * freq - PASSES)
    inside = (grid_row >= 0) & (grid_row < TH * n_pos) & (grid_col >= 0) & (grid_col < TILE_DEV * TW)
    inside = inside & (row16 < 3 * TH) & (lane16 < cols + 2 * PASSES)

    def widened(a):
        pieces = [strip[a * TH : (a + 1) * TH, :] for strip in strips]
        tall = jnp.concatenate(pieces + [pieces[0]], axis=0)
        return jnp.where(inside, tall, 0.0)

    across_k = widened(0)
    along_k = widened(1)
    ground = widened(2)
    south_k = jnp.minimum(across_k, pltpu.roll(across_k, 15, 0))
    north_k = jnp.minimum(across_k, pltpu.roll(across_k, 1, 0))
    east_k = jnp.minimum(along_k, pltpu.roll(along_k, LANES - 1, 1))
    west_k = jnp.minimum(along_k, pltpu.roll(along_k, 1, 1))

    slot_load.wait()

    def owner_copy(step, h):
        target = lax.rem(pos + step, n_pos)
        return pltpu.make_async_remote_copy(
            src_ref=packed.at[h, pl.ds(target * CAP, CAP)],
            dst_ref=arrived.at[h, pl.ds(pos * CAP, CAP)],
            send_sem=a2a_send.at[h, step],
            recv_sem=a2a_recv.at[h, step],
            device_id=(target, freq),
            device_id_type=MESH,
        )

    own_block = pl.ds(pos * CAP, CAP)
    own_copies = []
    for h in range(2):
        for own, (right, left) in (
            (messages, (messages - 4, messages - 1)),
            (messages + 1, (messages - 2, messages - 3)),
        ):
            ring_half(right, h).wait_recv()
            ring_half(left, h).wait_recv()
            p = ((own + 1) // 2) % 2
            done = send_b[own, h] + recv_b[right, h] + recv_b[left, h]
            for e in range(foot):
                final_b[h, p * foot + e] = done[e * TH : (e + 1) * TH, :]
        for slot in range(all_slots):
            packed[h, slot] = final_b[h, jnp.clip(slot_s[0, slot], 0, entries - 1)]

        @pl.loop(1, n_pos)
        def _(step):
            owner_copy(step, h).start()

        own_copy = pltpu.make_async_copy(
            packed.at[h, own_block], arrived.at[h, own_block], own_sem.at[h]
        )
        own_copy.start()
        own_copies.append(own_copy)

    compounds = []
    for h in range(2):

        @pl.loop(1, n_pos)
        def _(step):
            owner_copy(step, h).wait_recv()

        own_copies[h].wait()
        compound = None
        for piece in split3(arrived[h].reshape(spans, LANES)):
            part = jnp.dot(place, piece, preferred_element_type=jnp.float32)
            compound = part if compound is None else compound + part
        compounds.append(compound)
    compound = jnp.concatenate(compounds, axis=1)
    scaled = compound * compound * weight_v[...]
    energy = lax.dot_general(
        jnp.ones((8, rank), jnp.float32),
        scaled,
        (((1,), (1,)), ((), ())),
        precision=lax.Precision.HIGHEST,
        preferred_element_type=jnp.float32,
    )
    value_b[...] = jnp.sqrt(energy / rank + EPS)

    def value_copy(i, dp, df):
        return pltpu.make_async_remote_copy(
            src_ref=value_b,
            dst_ref=value_r.at[(1 - dp) * n_freq + freq],
            send_sem=val_send.at[i],
            recv_sem=val_recv.at[i],
            device_id=other(dp, df),
            device_id_type=MESH,
        )

    for i, (dp, df) in enumerate(near):
        value_copy(i, dp, df).start()

    value_r[n_freq + freq] = value_b[...]

    from_r = iota(jnp.int32, (LANES, TH * LANES), 0)
    to_n = iota(jnp.int32, (LANES, TH * LANES), 1)
    to_col = to_n % LANES + (cols * freq - PASSES) + TW
    chosen = (from_r // TILE_DEV == to_n // LANES) & (from_r % TILE_DEV == to_col // TW - 1)
    spread = jnp.where(chosen, 1.0, 0.0).astype(jnp.bfloat16)
    sub24 = iota(jnp.int32, (3 * TW, TH * LANES), 0)
    col24 = iota(jnp.int32, (3 * TW, TH * LANES), 1)
    keep = (col24 % LANES + (cols * freq - PASSES) + TW) % TW == sub24 % TW
    sub8 = iota(jnp.int32, (TW, LANES), 0)

    for i, (dp, df) in enumerate(near):
        value_copy(i, dp, df).wait_recv()

    groups = []
    for o in range(3):
        group = value_r[o * n_freq]
        for col in range(1, n_freq):
            group = jnp.where(sub8 == col, value_r[o * n_freq + col], group)
        groups.append(group)
    stacked = jnp.concatenate(groups, axis=0)
    wide = None
    for piece in split3(stacked):
        part = jnp.dot(piece, spread, preferred_element_type=jnp.float32)
        wide = part if wide is None else wide + part
    wide = jnp.where(keep, wide, 0.0)
    field = jnp.zeros((16, LANES), jnp.float32)
    for o in range(3):
        summed = jnp.sum(wide[o * TW : (o + 1) * TW, :], axis=0, keepdims=True)
        for r in range(TH):
            field = jnp.where(row16 == o * TH + r, summed[:, r * LANES : (r + 1) * LANES], field)
    u = jnp.where(inside, field + ground, 0.0)
    for sweep in range(PASSES):
        north = north_k * (pltpu.roll(u, 1, 0) - u)
        south = south_k * (pltpu.roll(u, 15, 0) - u)
        west = west_k * (pltpu.roll(u, 1, 1) - u)
        east = east_k * (pltpu.roll(u, LANES - 1, 1) - u)
        u = u + north + south + west + east
    u = pltpu.roll(u, LANES - PASSES, 1)
    out_ref[...] = u[TH : 2 * TH, :cols]

    @pl.loop(0, messages - 4)
    def _(u):
        ring_copy(u).wait_send()

    for h in range(2):

        @pl.loop(messages - 4, messages)
        def _(u):
            ring_half(u, h).wait_send()

        @pl.loop(1, n_pos)
        def _(step):
            owner_copy(step, h).wait_send()

    for i, (dp, df) in enumerate(halo_peers):
        halo_copy(i, dp, df).wait_send()
    for i, (dp, df) in enumerate(near):
        value_copy(i, dp, df).wait_send()


def body(footprint, basis, weights, conduct, baseline):
    pos_local, freq_local, doubled, rank = basis.shape
    foot = footprint.shape[1]
    n_pos = lax.axis_size("pos")
    n_freq = lax.axis_size("freq")
    rows = foot * TH
    entries = pos_local * foot
    slots = n_pos * CAP
    messages = 2 * n_freq - 2
    near = 3 * n_freq - 1
    hbm = pl.BlockSpec(memory_space=pltpu.MemorySpace.HBM)
    f32, bf16 = jnp.float32, jnp.bfloat16
    return pl.pallas_call(
        functools.partial(kernel, n_pos, n_freq),
        out_shape=jax.ShapeDtypeStruct(baseline.shape, f32),
        in_specs=[hbm] * 5,
        out_specs=pl.BlockSpec(memory_space=pltpu.VMEM),
        scratch_shapes=[
            pltpu.VMEM(footprint.shape[::-1], jnp.int32),
            pltpu.VMEM((1, rank), f32),
            pltpu.VMEM(conduct.shape, f32),
            pltpu.VMEM(baseline.shape, f32),
            pltpu.VMEM((pos_local, rows, LANES), f32),
            pltpu.VMEM((pos_local, rows, LANES), f32),
            pltpu.VMEM(basis.shape, bf16),
            pltpu.VMEM((doubled // 2 // LANES, freq_local, rows, 2 * LANES), bf16),
            pltpu.VMEM((messages + 2, 2, rows, LANES), f32),
            pltpu.VMEM((messages, 2, rows, LANES), f32),
            pltpu.VMEM((2, entries, TH, LANES), f32),
            pltpu.VMEM((2, slots, TH, LANES), f32),
            pltpu.VMEM((2, slots, TH, LANES), f32),
            pltpu.VMEM((8, LANES), f32),
            pltpu.VMEM((3 * n_freq, 8, LANES), f32),
            pltpu.VMEM((16, LANES), f32),
            pltpu.VMEM((9, 16, LANES), f32),
            pltpu.VMEM((1, slots), jnp.int32),
            pltpu.SMEM((1, slots), jnp.int32),
            pltpu.SemaphoreType.DMA((4,)),
            pltpu.SemaphoreType.DMA((pos_local,)),
            pltpu.SemaphoreType.DMA((messages, 2)),
            pltpu.SemaphoreType.DMA((messages, 2)),
            pltpu.SemaphoreType.DMA((3,)),
            pltpu.SemaphoreType.DMA((2, n_pos)),
            pltpu.SemaphoreType.DMA((2, n_pos)),
            pltpu.SemaphoreType.DMA((near,)),
            pltpu.SemaphoreType.DMA((near,)),
            pltpu.SemaphoreType.DMA((8,)),
            pltpu.SemaphoreType.DMA((9,)),
        ],
        compiler_params=pltpu.CompilerParams(
            collective_id=0, has_side_effects=True, vmem_limit_bytes=62 * 1024 * 1024
        ),
    )(footprint.T, weights.reshape(1, rank), conduct, baseline, basis)


def solution(mesh):
    return jax.shard_map(
        body,
        mesh=mesh,
        in_specs=(P(), P("pos", "freq", None, None), P(), P(None, "pos", "freq"), P("pos", "freq")),
        out_specs=P("pos", "freq"),
        check_vma=False,
    )
```

time: 63.8 us -> 54.1 us (0.85)
  local copies, waits for them, and re-layouts: 5.27 us -> 1.26 us
  Pallas kernels: 56.5 us -> 52.7 us
  other arithmetic: 1.54 us -> 0 us
    pallas_call x1, Pallas kernels: 56.5 us -> 52.7 us  [body(): pl.pallas_call(functools.partial(kernel, n_pos, n_freq), out_shape=jax.Sh...]
    unnamed x6 -> x1, local copies, waits for them, and re-layouts: 4.25 us -> 1.26 us
    concatenate x1 -> x0, other arithmetic: 0.71 us -> none  [body(): halo = jnp.concatenate([conduct.reshape(2 * TH, cols), baseline], axis=0)]
where the time goes in v2:
time: 54.1 us; the launch traced here: 53.9 us
  Pallas kernels  52.7 us (97%)
  local copies, waits for them, and re-layouts  1.26 us (2%)
    pallas_call x1, Pallas kernels, body(): pl.pallas_call(functools.partial(kernel, n_pos, n_freq), out_shape=jax.Sh...  52.7 us
    unnamed x1, local copies, waits for them, and re-layouts  1.26 us

profile of v2, /device:TPU:1, one launch (start us, length us, event | category | flops | bytes accessed | tf_op | source)
XLA Modules:
  0.0 53.9 jit_solution(12150248228524283843)
XLA Ops:
  0.0 52.7 %shard_map.55 = f32[4,32]{1,0:T(4,128)} custom-call(s32[32,64]{1,0:T(8,128)} %bitcast.2, f32[1,256]{1,0:T(1,128)} %bitcast.3, f32[2,4,32]{2,1,0:T(4,128)} %conduct_ref.1, f32[4,32]{1,0:T(4,128)} %base_ref.1, bf16[2,2,2048,256]{3,2,1,0:T(8,128)(2,1)} %basis_ref.1), custom_call_target="tpu_custom_call" | custom-call | tf_op jit(solution)/shard_map/pallas_call | solution.py:541
  52.7 1.3 %copy.7 = f32[4,32]{1,0:T(4,128)} copy(f32[4,32]{1,0:T(4,128)} %shard_map.55) | data formatting | bytes 1024

commit v3 on v2

v3 whole, which is shorter than its diff:
```python
import functools

import jax
import jax.numpy as jnp
from jax import lax
from jax.experimental import pallas as pl
from jax.experimental.pallas import tpu as pltpu
from jax.sharding import PartitionSpec as P

TH = 4
TW = 8
CELLS = TH * TW
TILE_DEV = 32
PASSES = 3
CAP = 4
EPS = 1e-06
MESH = pl.DeviceIdType.MESH

UNIT = 0.025
CELL = 28
PITCH = 5
TOP = 160
SIN_POLY = (-4.547240826688576, 9.23637803174852, -5.615372827081364)
SCALE_SQ = 0.6259964781564749
DOUBLE = (2.0 + 1e-6) / SCALE_SQ
LANES = 128


def green_block(cross, depth_sq, turns):
    square = cross * cross + depth_sq
    dist = square * lax.rsqrt(square)
    root = lax.rsqrt(dist)
    amp = root * (TOP**0.5)
    scaled_amp = root * (TOP**0.5 * SCALE_SQ)
    out = []
    for rate in turns:
        phase = dist * rate
        x = jnp.round(phase) - phase
        z = x * x
        s = x * (((z + SIN_POLY[0]) * z + SIN_POLY[1]) * z + SIN_POLY[2])
        w = DOUBLE - s * s
        u = w * scaled_amp
        out.append(((u - amp).astype(jnp.bfloat16), (u * s * lax.rsqrt(w)).astype(jnp.bfloat16)))
    return out


def make_unit(lat_ref, dep_ref, basis_v, green_s, rates, elements):
    rows = lat_ref.shape[1]

    def unit(col, p):
        total = None
        for tile in range(elements // LANES):
            start = tile * LANES
            shift = (2 * CELL * col + (PITCH * (elements - 1) - 2 * PITCH * start)).astype(jnp.float32) * 0.5
            for rg in range(rows // 16):
                span = pl.ds(rg * 16, 16)
                values = green_block(lat_ref[p, span, :] + shift, dep_ref[p, span, :], rates)
                for f, (cosine, sine) in enumerate(values):
                    green_s[tile, f, span, 0:LANES] = cosine
                    green_s[tile, f, span, LANES : 2 * LANES] = sine
            for f in range(len(rates)):
                right = jnp.concatenate(
                    [
                        basis_v[p, f, start : start + LANES, :],
                        basis_v[p, f, elements + start : elements + start + LANES, :],
                    ],
                    axis=0,
                )
                part = jnp.dot(green_s[tile, f], right, preferred_element_type=jnp.float32)
                total = part if total is None else total + part
        return total

    return unit


def split3(x):
    hi = x.astype(jnp.bfloat16)
    rest = x - hi.astype(jnp.float32)
    mid = rest.astype(jnp.bfloat16)
    low = (rest - mid.astype(jnp.float32)).astype(jnp.bfloat16)
    return hi, mid, low


PARTS = 4


def digits_of(n_pos):
    return {32: (4, 4, 2), 8: (2, 2, 2)}[n_pos]


def displaced(pos, n_pos, k):
    target = 0
    below = n_pos
    for size in digits_of(n_pos):
        below = below // size
        digit = lax.rem(pos // below, size)
        turn = lax.rem(k // below, size)
        if size == 4:
            move = jnp.where(turn == 0, 2, jnp.where(turn == 1, 1, jnp.where(turn == 2, 3, 0)))
        else:
            move = size - 1 - turn
        target = target * size + lax.rem(digit + move, size)
    return target


def kernel(
    n_pos,
    n_freq,
    foot_ref,
    weight_ref,
    conduct_ref,
    base_ref,
    basis_ref,
    out_ref,
    lat_v,
    dep_v,
    basis_v,
    green_s,
    send_b,
    recv_b,
    packed,
    arrived,
    value_b,
    value_r,
    halo_b,
    halo_r,
    basis_sem,
    ring_send,
    ring_recv,
    own_sem,
    a2a_send,
    a2a_recv,
    val_send,
    val_recv,
    halo_send,
    halo_recv,
):
    pos = lax.axis_index("pos")
    freq = lax.axis_index("freq")
    pos_local, freq_local, doubled, rank = basis_ref.shape
    elements = doubled // 2
    freqs = freq_local * n_freq
    foot = foot_ref.shape[0]
    rows = foot * TH
    pair = rows // 2
    entries = pos_local * foot
    positions = pos_local * n_pos
    half = n_freq // 2
    messages = 4 * half - 2
    iota = lax.broadcasted_iota
    f32, bf16, i32 = jnp.float32, jnp.bfloat16, jnp.int32

    basis_loads = [
        [
            pltpu.make_async_copy(basis_ref.at[p, f], basis_v.at[p, f], basis_sem.at[p, f])
            for f in range(freq_local)
        ]
        for p in range(pos_local)
    ]
    for p in range(pos_local):
        for copy in basis_loads[p]:
            copy.start()

    def other(dp, df):
        return (lax.rem(pos + dp + n_pos, n_pos), lax.rem(freq + df + n_freq, n_freq))

    barrier = pltpu.get_barrier_semaphore()
    near = [(dp, df) for dp in (-1, 0, 1) for df in range(n_freq) if (dp, df) != (0, 0)]
    near.sort(key=lambda d: -min(d[1], n_freq - d[1]) - abs(d[0]) * 0.5)
    sideways = [(dp, df) for dp, df in near if df != 0]
    for dp, df in sideways:
        pl.semaphore_signal(barrier, inc=1, device_id=other(dp, df), device_id_type=MESH)

    @pl.loop(0, n_pos - 1)
    def _(k):
        pl.semaphore_signal(
            barrier, inc=1, device_id=(displaced(pos, n_pos, k), freq), device_id_type=MESH
        )

    expand = iota(i32, (rows, foot), 0) % foot == iota(i32, (rows, foot), 1)
    expand = jnp.where(expand, 1.0, 0.0).astype(bf16)
    foot_all = foot_ref[...]
    foot_owner = (foot_all // TILE_DEV).astype(f32)
    foot_local = (foot_all % TILE_DEV).astype(f32)
    owner_of = jnp.dot(expand, foot_owner.astype(bf16), preferred_element_type=f32)
    local_of = jnp.dot(expand, foot_local.astype(bf16), preferred_element_type=f32)
    corner = iota(i32, (rows, 1), 0) // foot
    which = iota(i32, (rows, positions), 1)

    def locate(p):
        position = pos * pos_local + p
        owner = jnp.sum(jnp.where(which == position, owner_of, 0.0), axis=1, keepdims=True)
        local = jnp.sum(jnp.where(which == position, local_of, 0.0), axis=1, keepdims=True)
        depth = (TOP + CELL * (owner.astype(i32) * TH + corner)).astype(f32)
        centre = position * (CELL * TW * TILE_DEV // positions)
        lateral = CELL * TW * local.astype(i32) - centre
        lat_v[p] = (lateral - PITCH * iota(i32, (rows, LANES), 1)).astype(f32)
        dep_v[p] = jnp.broadcast_to(depth * depth, (rows, LANES))

    locate(0)

    rates = [
        (freqs // 2 + freq * freq_local + f).astype(f32) * (UNIT / freqs) for f in range(freq_local)
    ]
    unit = make_unit(lat_v, dep_v, basis_v, green_s, rates, elements)

    def compute(u):
        way = 1 - 2 * lax.rem(u, 2)
        dist = half - (u + 2) // 4
        p = lax.rem((u + 1) // 2, 2)
        done = unit(lax.rem(freq + way * dist + n_freq, n_freq), p)
        for h in range(2):
            send_b[u, h] = done[:, h * LANES : (h + 1) * LANES]

    def ring_copy(u):
        return pltpu.make_async_remote_copy(
            src_ref=send_b.at[u],
            dst_ref=recv_b.at[u],
            send_sem=ring_send.at[u, 0],
            recv_sem=ring_recv.at[u, 0],
            device_id=other(0, 1 - 2 * lax.rem(u, 2)),
            device_id_type=MESH,
        )

    def ring_part(u, c):
        span = pl.ds((c % 2) * pair, pair)
        return pltpu.make_async_remote_copy(
            src_ref=send_b.at[u, c // 2, span, :],
            dst_ref=recv_b.at[u, c // 2, span, :],
            send_sem=ring_send.at[u, c],
            recv_sem=ring_recv.at[u, c],
            device_id=other(0, 1 - 2 * lax.rem(u, 2)),
            device_id_type=MESH,
        )

    for copy in basis_loads[0]:
        copy.wait()
    compute(jnp.int32(0))
    pl.semaphore_wait(barrier, len(sideways) + n_pos - 1)
    ring_copy(0).start()
    for p in range(1, pos_local):
        locate(p)

    cols = base_ref.shape[1]
    halo_b[...] = jnp.zeros(halo_b.shape, f32)
    halo_b[0:TH, 0:cols] = conduct_ref[0]
    halo_b[TH : 2 * TH, 0:cols] = conduct_ref[1]
    halo_b[2 * TH : 3 * TH, 0:cols] = base_ref[...]
    halo_peers = [(dp, df) for dp in (-1, 0, 1) for df in (-1, 0, 1) if (dp, df) != (0, 0)]

    def halo_copy(i, dp, df):
        return pltpu.make_async_remote_copy(
            src_ref=halo_b,
            dst_ref=halo_r.at[(1 - dp) * 3 + (1 - df)],
            send_sem=halo_send.at[i],
            recv_sem=halo_recv.at[(1 - dp) * 3 + (1 - df)],
            device_id=other(dp, df),
            device_id_type=MESH,
        )

    @pl.loop(1, messages + 2)
    def _(u):
        @pl.when(u == 1)
        def _():
            for p in range(1, pos_local):
                for copy in basis_loads[p]:
                    copy.wait()

        compute(u)

        @pl.when((u >= 4) & (u < messages))
        def _():
            ring_copy(u - 4).wait_recv()
            send_b[u] += recv_b[u - 4]

        @pl.when(u < messages - 4)
        def _():
            ring_copy(u).start()

        @pl.when((u >= messages - 4) & (u < messages))
        def _():
            ring_part(u, 0).start()
            ring_part(u, 1).start()

        @pl.when((u >= messages - 2) & (u < messages))
        def _():
            for c in range(2, PARTS):
                ring_part(u - 2, c).start()
                ring_part(u, c).start()

        @pl.when(u == 5)
        def _():
            for i, (dp, df) in enumerate(halo_peers):
                halo_copy(i, dp, df).start()

    outs = n_pos * CAP * 2
    width = pos_local * 2 * foot
    picks = iota(i32, (foot, positions), 1)
    owner_col = jnp.concatenate(
        [
            jnp.sum(jnp.where(picks == pos * pos_local + p, foot_owner, 0.0), axis=1, keepdims=True)
            for p in range(pos_local)
        ],
        axis=0,
    )
    lane = iota(i32, (entries, width), 1)
    entry_of_lane = lane // (2 * foot) * foot + lane % foot
    entry = iota(i32, (entries, width), 0)
    owner_row = jnp.sum(jnp.where(entry == entry_of_lane, owner_col, 0.0), axis=0, keepdims=True)
    same = (owner_col == owner_row) & (entry < entry_of_lane)
    order_row = jnp.sum(jnp.where(same, 1.0, 0.0), axis=0, keepdims=True)
    slot_row = owner_row * CAP + order_row
    to_row = iota(i32, (outs, width), 0)
    from_lane = iota(i32, (outs, width), 1)
    slot_out = (to_row // (2 * CAP) * CAP + to_row % CAP).astype(f32)
    gather = (slot_out == slot_row) & (to_row // CAP % 2 == from_lane // foot % 2)
    gather = jnp.where(gather, 1.0, 0.0).astype(bf16)
    gather = jnp.concatenate([gather] * 3, axis=1)

    mine = foot_owner == pos.astype(f32)
    mine_b = jnp.where(mine, 1.0, 0.0).astype(bf16)
    lower = iota(i32, (foot, foot), 1) < iota(i32, (foot, foot), 0)
    from_p = iota(i32, (positions, positions), 0)
    to_p = iota(i32, (positions, positions), 1)
    later = (from_p // pos_local == to_p // pos_local) & (from_p < to_p)
    moved = jnp.dot(mine_b, jnp.where(later, 1.0, 0.0).astype(bf16), preferred_element_type=f32)
    ahead = jnp.dot(
        jnp.where(lower, 1.0, 0.0).astype(bf16), mine_b, preferred_element_type=f32
    ) + jnp.sum(moved, axis=0, keepdims=True)
    found = jnp.concatenate(
        [
            jnp.sum(jnp.where(mine & (ahead == s), foot_local + 1.0, 0.0), axis=0, keepdims=True)
            for s in range(CAP)
        ],
        axis=0,
    )
    block_of = iota(i32, (positions, outs), 0) // pos_local
    block_to = iota(i32, (positions, outs), 1) // (2 * CAP)
    table = jnp.dot(
        found.astype(bf16),
        jnp.where(block_of == block_to, 1.0, 0.0).astype(bf16),
        preferred_element_type=f32,
    )
    turn = iota(i32, (CAP, outs), 1) % CAP == iota(i32, (CAP, outs), 0)
    tile_in = jnp.sum(jnp.where(turn, table, 0.0), axis=0, keepdims=True)
    row_in = iota(i32, (1, outs), 1) // CAP % 2
    target_row = jnp.where(tile_in > 0.0, tile_in - 1.0 + (TILE_DEV * row_in).astype(f32), -1.0)
    place = iota(i32, (2 * TILE_DEV, outs), 0).astype(f32) == target_row
    place = jnp.where(place, 1.0, 0.0).astype(bf16)
    place = jnp.concatenate([place] * 3, axis=1)

    for i, (dp, df) in enumerate(halo_peers):
        halo_copy(i, dp, df).wait_recv()
    lane16 = iota(i32, (16, LANES), 1)
    row16 = iota(i32, (16, LANES), 0)
    strips = []
    for dp in (-1, 0, 1):
        left = halo_r[(dp + 1) * 3]
        centre = halo_b[...] if dp == 0 else halo_r[(dp + 1) * 3 + 1]
        right = halo_r[(dp + 1) * 3 + 2]
        strip = jnp.where(
            lane16 < PASSES,
            pltpu.roll(left, LANES - cols + PASSES, 1),
            jnp.where(
                lane16 < cols + PASSES,
                pltpu.roll(centre, PASSES, 1),
                pltpu.roll(right, cols + PASSES, 1),
            ),
        )
        strips.append(strip)
    grid_row = row16 + TH * (pos - 1)
    grid_col = lane16 + (cols * freq - PASSES)
    inside = (grid_row >= 0) & (grid_row < TH * n_pos) & (grid_col >= 0) & (grid_col < TILE_DEV * TW)
    inside = inside & (row16 < 3 * TH) & (lane16 < cols + 2 * PASSES)

    def widened(a):
        pieces = [strip[a * TH : (a + 1) * TH, :] for strip in strips]
        tall = jnp.concatenate(pieces + [pieces[0]], axis=0)
        return jnp.where(inside, tall, 0.0)

    across_k = widened(0)
    along_k = widened(1)
    ground = widened(2)
    south_k = jnp.minimum(across_k, pltpu.roll(across_k, 15, 0))
    north_k = jnp.minimum(across_k, pltpu.roll(across_k, 1, 0))
    east_k = jnp.minimum(along_k, pltpu.roll(along_k, LANES - 1, 1))
    west_k = jnp.minimum(along_k, pltpu.roll(along_k, 1, 1))

    block = 2 * CAP

    def owner_copy(k, c):
        target = displaced(pos, n_pos, k)
        return pltpu.make_async_remote_copy(
            src_ref=packed.at[c, pl.ds(pl.multiple_of(target * block, block), block), :],
            dst_ref=arrived.at[c, pl.ds(pl.multiple_of(pos * block, block), block), :],
            send_sem=a2a_send.at[c, k],
            recv_sem=a2a_recv.at[c, k],
            device_id=(target, freq),
            device_id_type=MESH,
        )

    own_block = pl.ds(pl.multiple_of(pos * block, block), block)
    own_copies = []
    for c in range(PARTS):
        span = pl.ds((c % 2) * pair, pair)
        sums = []
        for own, right, left in (
            (messages + 1, messages - 2, messages - 3),
            (messages, messages - 4, messages - 1),
        ):
            ring_part(right, c).wait_recv()
            ring_part(left, c).wait_recv()
            sums.append(send_b[own, c // 2, span, :] + recv_b[right, c // 2, span, :] + recv_b[left, c // 2, span, :])
        stacked = jnp.concatenate(split3(jnp.concatenate(sums, axis=0)), axis=0)
        packed[c] = jnp.dot(gather, stacked, preferred_element_type=f32)

        @pl.loop(0, n_pos - 1)
        def _(k):
            owner_copy(k, c).start()

        own_copy = pltpu.make_async_copy(
            packed.at[c, own_block, :], arrived.at[c, own_block, :], own_sem.at[c]
        )
        own_copy.start()
        own_copies.append(own_copy)

    energies = [None, None]
    for c in range(PARTS):

        @pl.loop(0, n_pos - 1)
        def _(k):
            owner_copy(k, c).wait_recv()

        own_copies[c].wait()
        stacked = jnp.concatenate(split3(arrived[c]), axis=0)
        compound = jnp.dot(place, stacked, preferred_element_type=f32)
        scaled = compound * compound * weight_ref[0:1, (c // 2) * LANES : (c // 2 + 1) * LANES]
        energies[c % 2] = scaled if energies[c % 2] is None else energies[c % 2] + scaled
    value = jnp.zeros((1, LANES), f32)
    for pair_at, energy in enumerate(energies):
        energy = jnp.sum(energy, axis=1, keepdims=True)
        on = iota(i32, (2 * TILE_DEV, LANES), 1) == iota(i32, (2 * TILE_DEV, LANES), 0) + pair_at * 2 * TILE_DEV
        value = value + jnp.sum(jnp.where(on, energy, 0.0), axis=0, keepdims=True)
    value_b[...] = jnp.sqrt(value / rank + EPS)

    def value_copy(i, dp, df):
        return pltpu.make_async_remote_copy(
            src_ref=value_b,
            dst_ref=value_r.at[(1 - dp) * n_freq + freq],
            send_sem=val_send.at[i],
            recv_sem=val_recv.at[i],
            device_id=other(dp, df),
            device_id_type=MESH,
        )

    for i, (dp, df) in enumerate(near):
        value_copy(i, dp, df).start()

    value_r[n_freq + freq] = value_b[...]

    @pl.loop(0, messages - 4)
    def _(u):
        ring_copy(u).wait_send()

    for c in range(PARTS):

        @pl.loop(messages - 4, messages)
        def _(u):
            ring_part(u, c).wait_send()

        @pl.loop(0, n_pos - 1)
        def _(k):
            owner_copy(k, c).wait_send()

    for i, (dp, df) in enumerate(halo_peers):
        halo_copy(i, dp, df).wait_send()

    from_r = iota(i32, (LANES, TH * LANES), 0)
    to_n = iota(i32, (LANES, TH * LANES), 1)
    to_col = to_n % LANES + (cols * freq - PASSES) + TW
    chosen = (from_r // TILE_DEV == to_n // LANES) & (from_r % TILE_DEV == to_col // TW - 1)
    spread = jnp.where(chosen, 1.0, 0.0).astype(bf16)
    sub24 = iota(i32, (3 * TW, TH * LANES), 0)
    col24 = iota(i32, (3 * TW, TH * LANES), 1)
    keep = (col24 % LANES + (cols * freq - PASSES) + TW) % TW == sub24 % TW
    sub8 = iota(i32, (TW, LANES), 0)

    for i, (dp, df) in enumerate(near):
        value_copy(i, dp, df).wait_recv()

    groups = []
    for o in range(3):
        group = jnp.broadcast_to(value_r[o * n_freq], (TW, LANES))
        for col in range(1, n_freq):
            group = jnp.where(sub8 == col, value_r[o * n_freq + col], group)
        groups.append(group)
    wide = None
    for piece in split3(jnp.concatenate(groups, axis=0)):
        part = jnp.dot(piece, spread, preferred_element_type=f32)
        wide = part if wide is None else wide + part
    wide = jnp.where(keep, wide, 0.0)
    field = jnp.zeros((16, LANES), f32)
    for o in range(3):
        summed = jnp.sum(wide[o * TW : (o + 1) * TW, :], axis=0, keepdims=True)
        for r in range(TH):
            field = jnp.where(row16 == o * TH + r, summed[:, r * LANES : (r + 1) * LANES], field)
    u = jnp.where(inside, field + ground, 0.0)
    for sweep in range(PASSES):
        north = north_k * (pltpu.roll(u, 1, 0) - u)
        south = south_k * (pltpu.roll(u, 15, 0) - u)
        west = west_k * (pltpu.roll(u, 1, 1) - u)
        east = east_k * (pltpu.roll(u, LANES - 1, 1) - u)
        u = u + north + south + west + east
    u = pltpu.roll(u, LANES - PASSES, 1)
    out_ref[...] = u[TH : 2 * TH, :cols]

    for i, (dp, df) in enumerate(near):
        value_copy(i, dp, df).wait_send()


def body(footprint, basis, weights, conduct, baseline):
    pos_local, freq_local, doubled, rank = basis.shape
    foot = footprint.shape[1]
    n_pos = lax.axis_size("pos")
    n_freq = lax.axis_size("freq")
    rows = foot * TH
    outs = n_pos * CAP * 2
    messages = 2 * n_freq - 2
    near = 3 * n_freq - 1
    vmem = pl.BlockSpec(memory_space=pltpu.VMEM)
    hbm = pl.BlockSpec(memory_space=pltpu.MemorySpace.HBM)
    f32, bf16 = jnp.float32, jnp.bfloat16
    return pl.pallas_call(
        functools.partial(kernel, n_pos, n_freq),
        out_shape=jax.ShapeDtypeStruct(baseline.shape, f32),
        in_specs=[vmem] * 4 + [hbm],
        out_specs=vmem,
        scratch_shapes=[
            pltpu.VMEM((pos_local, rows, LANES), f32),
            pltpu.VMEM((pos_local, rows, LANES), f32),
            pltpu.VMEM(basis.shape, bf16),
            pltpu.VMEM((doubled // 2 // LANES, freq_local, rows, 2 * LANES), bf16),
            pltpu.VMEM((messages + 2, 2, rows, LANES), f32),
            pltpu.VMEM((messages, 2, rows, LANES), f32),
            pltpu.VMEM((PARTS, outs, LANES), f32),
            pltpu.VMEM((PARTS, outs, LANES), f32),
            pltpu.VMEM((1, LANES), f32),
            pltpu.VMEM((3 * n_freq, 1, LANES), f32),
            pltpu.VMEM((16, LANES), f32),
            pltpu.VMEM((9, 16, LANES), f32),
            pltpu.SemaphoreType.DMA((pos_local, freq_local)),
            pltpu.SemaphoreType.DMA((messages, PARTS)),
            pltpu.SemaphoreType.DMA((messages, PARTS)),
            pltpu.SemaphoreType.DMA((PARTS,)),
            pltpu.SemaphoreType.DMA((PARTS, n_pos)),
            pltpu.SemaphoreType.DMA((PARTS, n_pos)),
            pltpu.SemaphoreType.DMA((near,)),
            pltpu.SemaphoreType.DMA((near,)),
            pltpu.SemaphoreType.DMA((8,)),
            pltpu.SemaphoreType.DMA((9,)),
        ],
        compiler_params=pltpu.CompilerParams(
            collective_id=0, has_side_effects=True, vmem_limit_bytes=50 * 1024 * 1024
        ),
    )(footprint.T, weights.reshape(1, rank), conduct, baseline, basis)


def solution(mesh):
    return jax.shard_map(
        body,
        mesh=mesh,
        in_specs=(P(), P("pos", "freq", None, None), P(), P(None, "pos", "freq"), P("pos", "freq")),
        out_specs=P("pos", "freq"),
        check_vma=False,
    )
```

time: 54.1 us -> 54.4 us (level)
  local copies, waits for them, and re-layouts: 1.26 us -> 3.34 us
  Pallas kernels: 52.7 us -> 50.8 us
    unnamed x1 -> x9, local copies, waits for them, and re-layouts: 1.26 us -> 3.34 us
    pallas_call x1, Pallas kernels: 52.7 us -> 50.8 us  [body(): pl.pallas_call(functools.partial(kernel, n_pos, n_freq), out_shape=jax.Sh...]
where the time goes in v3:
time: 54.4 us; the launch traced here: 54.1 us
  Pallas kernels  50.8 us (93%)
  local copies, waits for them, and re-layouts  3.34 us (6%)
    pallas_call x1, Pallas kernels, body(): pl.pallas_call(functools.partial(kernel, n_pos, n_freq), out_shape=jax.Sh...  50.8 us
    unnamed x9, local copies, waits for them, and re-layouts  3.34 us

profile of v3, /device:TPU:1, one launch (start us, length us, event | category | flops | bytes accessed | tf_op | source)
XLA Modules:
  0.0 54.1 jit_solution(10629748209114950619)
XLA Ops:
  0.0 0.0 copy-start
  0.0 0.7 %copy-done = s32[64,32]{0,1:T(8,128)S(1)} copy-done((s32[64,32]{0,1:T(8,128)S(1)}, s32[64,32]{0,1:T(8,128)}, u32[]{:S(2)}) %copy-start) | copy-done | bytes 8216
  0.7 0.0 copy-start.1
  0.7 0.7 %copy-done.1 = f32[2,4,32]{2,1,0:T(4,128)S(1)} copy-done((f32[2,4,32]{2,1,0:T(4,128)S(1)}, f32[2,4,32]{2,1,0:T(4,128)}, u32[]{:S(2)}) %copy-start.1) | copy-done | bytes 1048
  1.4 0.0 copy-start.2
  1.4 0.7 %copy-done.2 = f32[4,32]{1,0:T(4,128)S(1)} copy-done((f32[4,32]{1,0:T(4,128)S(1)}, f32[4,32]{1,0:T(4,128)}, u32[]{:S(2)}) %copy-start.2) | copy-done | bytes 536
  2.1 0.0 copy-start.3
  2.1 0.7 %copy-done.3 = f32[256]{0:T(256)S(1)} copy-done((f32[256]{0:T(256)S(1)}, f32[256]{0:T(256)}, u32[]{:S(2)}) %copy-start.3) | copy-done | bytes 1048
  2.8 50.8 %shard_map.55 = f32[4,32]{1,0:T(4,128)S(1)} custom-call(s32[32,64]{1,0:T(8,128)S(1)} %bitcast.2, f32[1,256]{1,0:T(1,128)S(1)} %bitcast.3, f32[2,4,32]{2,1,0:T(4,128)S(1)} %copy-done.1, f32[4,32]{1,0:T(4,128)S(1)} %copy-done.2, bf16[2,2,2048,256]{3,2,1,0:T(8,128)(2,1)} %basis_ref.1), custom_call_target="tpu_custom_call" | custom-call | tf_op jit(solution)/shard_map/pallas_call | solution.py:533
  53.6 0.6 %copy.7 = f32[4,32]{1,0:T(4,128)} copy(f32[4,32]{1,0:T(4,128)S(1)} %shard_map.55) | data formatting | bytes 1024
Async XLA Ops:
  0.0 0.7 %copy-start = (s32[64,32]{0,1:T(8,128)S(1)}, s32[64,32]{0,1:T(8,128)}, u32[]{:S(2)}) copy-start(s32[64,32]{0,1:T(8,128)} %param.5) | copy-start | bytes 24580
  0.7 0.7 %copy-start.1 = (f32[2,4,32]{2,1,0:T(4,128)S(1)}, f32[2,4,32]{2,1,0:T(4,128)}, u32[]{:S(2)}) copy-start(f32[2,4,32]{2,1,0:T(4,128)} %conduct_ref.1) | copy-start | bytes 3076
  1.4 0.7 %copy-start.2 = (f32[4,32]{1,0:T(4,128)S(1)}, f32[4,32]{1,0:T(4,128)}, u32[]{:S(2)}) copy-start(f32[4,32]{1,0:T(4,128)} %base_ref.1) | copy-start | bytes 1540
  2.1 0.7 %copy-start.3 = (f32[256]{0:T(256)S(1)}, f32[256]{0:T(256)}, u32[]{:S(2)}) copy-start(f32[256]{0:T(256)} %param.7) | copy-start | bytes 3076

commit v4 on v3

--- a/solution.py
+++ b/solution.py
@@ -1,4 +1,5 @@
 import functools
+import itertools
 
 import jax
 import jax.numpy as jnp
@@ -88,30 +89,33 @@
     return {32: (4, 4, 2), 8: (2, 2, 2)}[n_pos]
 
 
-def displaced(pos, n_pos, k):
-    target = 0
+def walks_of(pos, n_pos):
+    sizes = digits_of(n_pos)
+    tables = []
     below = n_pos
-    for size in digits_of(n_pos):
+    for size in sizes:
         below = below // size
-        digit = lax.rem(pos // below, size)
-        turn = lax.rem(k // below, size)
-        if size == 4:
-            move = jnp.where(turn == 0, 2, jnp.where(turn == 1, 1, jnp.where(turn == 2, 3, 0)))
-        else:
-            move = size - 1 - turn
-        target = target * size + lax.rem(digit + move, size)
-    return target
+        digit = pos // below % size
+        tables.append([(digit + move) % size * below for move in range(size)])
+    moves = list(itertools.product(*[range(size) for size in sizes]))[1:]
+    moves.sort(key=lambda m: -sum(min(d, z - d) for d, z in zip(m, sizes)))
+    return [sum(table[d] for table, d in zip(tables, m)) for m in moves]
 
 
 def kernel(
     n_pos,
     n_freq,
+    foot_in,
+    weight_in,
+    conduct_in,
+    base_in,
+    basis_ref,
+    out_ref,
     foot_ref,
     weight_ref,
     conduct_ref,
     base_ref,
-    basis_ref,
-    out_ref,
+    in_sem,
     lat_v,
     dep_v,
     basis_v,
@@ -127,7 +131,6 @@
     basis_sem,
     ring_send,
     ring_recv,
-    own_sem,
     a2a_send,
     a2a_recv,
     val_send,
@@ -157,12 +160,32 @@
         ]
         for p in range(pos_local)
     ]
+    foot_load, *small_loads = [
+        pltpu.make_async_copy(src, dst, in_sem.at[i])
+        for i, (src, dst) in enumerate(
+            (
+                (foot_in, foot_ref),
+                (conduct_in, conduct_ref),
+                (base_in, base_ref),
+                (weight_in, weight_ref),
+            )
+        )
+    ]
+    foot_load.start()
     for p in range(pos_local):
         for copy in basis_loads[p]:
             copy.start()
+    for copy in small_loads:
+        copy.start()
+
+    rows_at = {dp: (pos + dp + n_pos) % n_pos if dp else pos for dp in (-1, 0, 1)}
+    cols_at = [(freq + df) % n_freq for df in range(n_freq)]
 
     def other(dp, df):
-        return (lax.rem(pos + dp + n_pos, n_pos), lax.rem(freq + df + n_freq, n_freq))
+        return (rows_at[dp], cols_at[df % n_freq] if isinstance(df, int) else (freq + df + n_freq) % n_freq)
+
+    def wait_all(ref, sem):
+        pltpu.make_async_copy(ref, ref, sem).wait()
 
     barrier = pltpu.get_barrier_semaphore()
     near = [(dp, df) for dp in (-1, 0, 1) for df in range(n_freq) if (dp, df) != (0, 0)]
@@ -171,14 +194,13 @@
     for dp, df in sideways:
         pl.semaphore_signal(barrier, inc=1, device_id=other(dp, df), device_id_type=MESH)
 
-    @pl.loop(0, n_pos - 1)
-    def _(k):
-        pl.semaphore_signal(
-            barrier, inc=1, device_id=(displaced(pos, n_pos, k), freq), device_id_type=MESH
-        )
+    walks = walks_of(pos, n_pos)
+    for target in walks:
+        pl.semaphore_signal(barrier, inc=1, device_id=(target, freq), device_id_type=MESH)
 
     expand = iota(i32, (rows, foot), 0) % foot == iota(i32, (rows, foot), 1)
     expand = jnp.where(expand, 1.0, 0.0).astype(bf16)
+    foot_load.wait()
     foot_all = foot_ref[...]
     foot_owner = (foot_all // TILE_DEV).astype(f32)
     foot_local = (foot_all % TILE_DEV).astype(f32)
@@ -216,7 +238,7 @@
         return pltpu.make_async_remote_copy(
             src_ref=send_b.at[u],
             dst_ref=recv_b.at[u],
-            send_sem=ring_send.at[u, 0],
+            send_sem=ring_send,
             recv_sem=ring_recv.at[u, 0],
             device_id=other(0, 1 - 2 * lax.rem(u, 2)),
             device_id_type=MESH,
@@ -227,7 +249,7 @@
         return pltpu.make_async_remote_copy(
             src_ref=send_b.at[u, c // 2, span, :],
             dst_ref=recv_b.at[u, c // 2, span, :],
-            send_sem=ring_send.at[u, c],
+            send_sem=ring_send,
             recv_sem=ring_recv.at[u, c],
             device_id=other(0, 1 - 2 * lax.rem(u, 2)),
             device_id_type=MESH,
@@ -241,6 +263,8 @@
     for p in range(1, pos_local):
         locate(p)
 
+    for copy in small_loads:
+        copy.wait()
     cols = base_ref.shape[1]
     halo_b[...] = jnp.zeros(halo_b.shape, f32)
     halo_b[0:TH, 0:cols] = conduct_ref[0]
@@ -252,8 +276,8 @@
         return pltpu.make_async_remote_copy(
             src_ref=halo_b,
             dst_ref=halo_r.at[(1 - dp) * 3 + (1 - df)],
-            send_sem=halo_send.at[i],
-            recv_sem=halo_recv.at[(1 - dp) * 3 + (1 - df)],
+            send_sem=halo_send,
+            recv_sem=halo_recv,
             device_id=other(dp, df),
             device_id_type=MESH,
         )
@@ -349,8 +373,7 @@
     place = jnp.where(place, 1.0, 0.0).astype(bf16)
     place = jnp.concatenate([place] * 3, axis=1)
 
-    for i, (dp, df) in enumerate(halo_peers):
-        halo_copy(i, dp, df).wait_recv()
+    wait_all(halo_r.at[pl.ds(0, 8)], halo_recv)
     lane16 = iota(i32, (16, LANES), 1)
     row16 = iota(i32, (16, LANES), 0)
     strips = []
@@ -387,20 +410,18 @@
     west_k = jnp.minimum(along_k, pltpu.roll(along_k, 1, 1))
 
     block = 2 * CAP
-
-    def owner_copy(k, c):
-        target = displaced(pos, n_pos, k)
+    own_block = pl.ds(pl.multiple_of(pos * block, block), block)
+
+    def owner_copy(target, c):
         return pltpu.make_async_remote_copy(
             src_ref=packed.at[c, pl.ds(pl.multiple_of(target * block, block), block), :],
-            dst_ref=arrived.at[c, pl.ds(pl.multiple_of(pos * block, block), block), :],
-            send_sem=a2a_send.at[c, k],
-            recv_sem=a2a_recv.at[c, k],
+            dst_ref=arrived.at[c, own_block, :],
+            send_sem=a2a_send,
+            recv_sem=a2a_recv.at[c],
             device_id=(target, freq),
             device_id_type=MESH,
         )
 
-    own_block = pl.ds(pl.multiple_of(pos * block, block), block)
-    own_copies = []
     for c in range(PARTS):
         span = pl.ds((c % 2) * pair, pair)
         sums = []
@@ -414,24 +435,15 @@
         stacked = jnp.concatenate(split3(jnp.concatenate(sums, axis=0)), axis=0)
         packed[c] = jnp.dot(gather, stacked, preferred_element_type=f32)
 
-        @pl.loop(0, n_pos - 1)
-        def _(k):
-            owner_copy(k, c).start()
-
-        own_copy = pltpu.make_async_copy(
-            packed.at[c, own_block, :], arrived.at[c, own_block, :], own_sem.at[c]
-        )
-        own_copy.start()
-        own_copies.append(own_copy)
+        for target in walks:
+            owner_copy(target, c).start()
+        pltpu.make_async_copy(
+            packed.at[c, own_block, :], arrived.at[c, own_block, :], a2a_recv.at[c]
+        ).start()
 
     energies = [None, None]
     for c in range(PARTS):
-
-        @pl.loop(0, n_pos - 1)
-        def _(k):
-            owner_copy(k, c).wait_recv()
-
-        own_copies[c].wait()
+        wait_all(arrived.at[c], a2a_recv.at[c])
         stacked = jnp.concatenate(split3(arrived[c]), axis=0)
         compound = jnp.dot(place, stacked, preferred_element_type=f32)
         scaled = compound * compound * weight_ref[0:1, (c // 2) * LANES : (c // 2 + 1) * LANES]
@@ -447,8 +459,8 @@
         return pltpu.make_async_remote_copy(
             src_ref=value_b,
             dst_ref=value_r.at[(1 - dp) * n_freq + freq],
-            send_sem=val_send.at[i],
-            recv_sem=val_recv.at[i],
+            send_sem=val_send,
+            recv_sem=val_recv,
             device_id=other(dp, df),
             device_id_type=MESH,
         )
@@ -458,22 +470,9 @@
 
     value_r[n_freq + freq] = value_b[...]
 
-    @pl.loop(0, messages - 4)
-    def _(u):
-        ring_copy(u).wait_send()
-
-    for c in range(PARTS):
-
-        @pl.loop(messages - 4, messages)
-        def _(u):
-            ring_part(u, c).wait_send()
-
-        @pl.loop(0, n_pos - 1)
-        def _(k):
-            owner_copy(k, c).wait_send()
-
-    for i, (dp, df) in enumerate(halo_peers):
-        halo_copy(i, dp, df).wait_send()
+    wait_all(send_b.at[pl.ds(0, messages)], ring_send)
+    wait_all(packed.at[:, pl.ds(0, (n_pos - 1) * block), :], a2a_send)
+    wait_all(halo_r.at[pl.ds(0, 8)], halo_send)
 
     from_r = iota(i32, (LANES, TH * LANES), 0)
     to_n = iota(i32, (LANES, TH * LANES), 1)
@@ -485,8 +484,7 @@
     keep = (col24 % LANES + (cols * freq - PASSES) + TW) % TW == sub24 % TW
     sub8 = iota(i32, (TW, LANES), 0)
 
-    for i, (dp, df) in enumerate(near):
-        value_copy(i, dp, df).wait_recv()
+    wait_all(value_r.at[pl.ds(0, len(near))], val_recv)
 
     groups = []
     for o in range(3):
@@ -514,8 +512,7 @@
     u = pltpu.roll(u, LANES - PASSES, 1)
     out_ref[...] = u[TH : 2 * TH, :cols]
 
-    for i, (dp, df) in enumerate(near):
-        value_copy(i, dp, df).wait_send()
+    wait_all(value_r.at[pl.ds(0, len(near))], val_send)
 
 
 def body(footprint, basis, weights, conduct, baseline):
@@ -526,16 +523,20 @@
     rows = foot * TH
     outs = n_pos * CAP * 2
     messages = 2 * n_freq - 2
-    near = 3 * n_freq - 1
     vmem = pl.BlockSpec(memory_space=pltpu.VMEM)
     hbm = pl.BlockSpec(memory_space=pltpu.MemorySpace.HBM)
     f32, bf16 = jnp.float32, jnp.bfloat16
     return pl.pallas_call(
         functools.partial(kernel, n_pos, n_freq),
         out_shape=jax.ShapeDtypeStruct(baseline.shape, f32),
-        in_specs=[vmem] * 4 + [hbm],
+        in_specs=[hbm] * 5,
         out_specs=vmem,
         scratch_shapes=[
+            pltpu.VMEM(footprint.shape[::-1], jnp.int32),
+            pltpu.VMEM((1, rank), f32),
+            pltpu.VMEM(conduct.shape, f32),
+            pltpu.VMEM(baseline.shape, f32),
+            pltpu.SemaphoreType.DMA((4,)),
             pltpu.VMEM((pos_local, rows, LANES), f32),
             pltpu.VMEM((pos_local, rows, LANES), f32),
             pltpu.VMEM(basis.shape, bf16),
@@ -549,20 +550,19 @@
             pltpu.VMEM((16, LANES), f32),
             pltpu.VMEM((9, 16, LANES), f32),
             pltpu.SemaphoreType.DMA((pos_local, freq_local)),
+            pltpu.SemaphoreType.DMA,
             pltpu.SemaphoreType.DMA((messages, PARTS)),
-            pltpu.SemaphoreType.DMA((messages, PARTS)),
+            pltpu.SemaphoreType.DMA,
             pltpu.SemaphoreType.DMA((PARTS,)),
-            pltpu.SemaphoreType.DMA((PARTS, n_pos)),
-            pltpu.SemaphoreType.DMA((PARTS, n_pos)),
-            pltpu.SemaphoreType.DMA((near,)),
-            pltpu.SemaphoreType.DMA((near,)),
-            pltpu.SemaphoreType.DMA((8,)),
-            pltpu.SemaphoreType.DMA((9,)),
+            pltpu.SemaphoreType.DMA,
+            pltpu.SemaphoreType.DMA,
+            pltpu.SemaphoreType.DMA,
+            pltpu.SemaphoreType.DMA,
         ],
         compiler_params=pltpu.CompilerParams(
             collective_id=0, has_side_effects=True, vmem_limit_bytes=50 * 1024 * 1024
         ),
-    )(footprint.T, weights.reshape(1, rank), conduct, baseline, basis)
+    )(*[pltpu.with_memory_space_constraint(x, pltpu.MemorySpace.HBM) for x in (footprint.T, weights.reshape(1, rank), conduct, baseline, basis)])
 
 
 def solution(mesh):

time: 54.4 us -> 48 us (0.88)
  Pallas kernels: 50.8 us -> 47.2 us
  local copies, waits for them, and re-layouts: 3.34 us -> 0.58 us
    pallas_call x1, Pallas kernels: 50.8 us -> 47.2 us  [body(): pl.pallas_call(functools.partial(kernel, n_pos, n_freq), out_shape=jax.Sh...]
    unnamed x9 -> x1, local copies, waits for them, and re-layouts: 3.34 us -> 0.58 us
where the time goes in v4:
time: 48 us; the launch traced here: 47.8 us
  Pallas kernels  47.2 us (98%)
  local copies, waits for them, and re-layouts  0.58 us (1%)
    pallas_call x1, Pallas kernels, body(): pl.pallas_call(functools.partial(kernel, n_pos, n_freq), out_shape=jax.Sh...  47.2 us

profile of v4, /device:TPU:1, one launch (start us, length us, event | category | flops | bytes accessed | tf_op | source)
XLA Modules:
  0.0 47.8 jit_solution(6269995204229931107)
XLA Ops:
  0.0 47.2 %shard_map.55 = f32[4,32]{1,0:T(4,128)S(1)} custom-call(s32[32,64]{1,0:T(8,128)} %bitcast.2, f32[1,256]{1,0:T(1,128)} %bitcast.3, f32[2,4,32]{2,1,0:T(4,128)} %conduct_in.1, f32[4,32]{1,0:T(4,128)} %base_in.1, bf16[2,2,2048,256]{3,2,1,0:T(8,128)(2,1)} %basis_ref.1), custom_call_target="tpu_custom_call" | custom-call | tf_op jit(solution)/shard_map/pallas_call | solution.py:529
  47.3 0.6 %copy.7 = f32[4,32]{1,0:T(4,128)} copy(f32[4,32]{1,0:T(4,128)S(1)} %shard_map.55) | data formatting | bytes 1024

commit v5 on v4

--- a/solution.py
+++ b/solution.py
@@ -48,12 +48,12 @@
 def make_unit(lat_ref, dep_ref, basis_v, green_s, rates, elements):
     rows = lat_ref.shape[1]
 
-    def unit(col, p):
+    def unit(col, p, base=0, height=rows):
         total = None
         for tile in range(elements // LANES):
             start = tile * LANES
             shift = (2 * CELL * col + (PITCH * (elements - 1) - 2 * PITCH * start)).astype(jnp.float32) * 0.5
-            for rg in range(rows // 16):
+            for rg in range(base // 16, (base + height) // 16):
                 span = pl.ds(rg * 16, 16)
                 values = green_block(lat_ref[p, span, :] + shift, dep_ref[p, span, :], rates)
                 for f, (cosine, sine) in enumerate(values):
@@ -67,7 +67,9 @@
                     ],
                     axis=0,
                 )
-                part = jnp.dot(green_s[tile, f], right, preferred_element_type=jnp.float32)
+                part = jnp.dot(
+                    green_s[tile, f, base : base + height, :], right, preferred_element_type=jnp.float32
+                )
                 total = part if total is None else total + part
         return total
 
@@ -226,13 +228,13 @@
     ]
     unit = make_unit(lat_v, dep_v, basis_v, green_s, rates, elements)
 
-    def compute(u):
-        way = 1 - 2 * lax.rem(u, 2)
+    def compute(u, base=0, height=rows):
+        way = 1 - 2 * (u % 2)
         dist = half - (u + 2) // 4
-        p = lax.rem((u + 1) // 2, 2)
-        done = unit(lax.rem(freq + way * dist + n_freq, n_freq), p)
+        p = (u + 1) // 2 % 2
+        done = unit((freq + way * dist + n_freq) % n_freq, p, base, height)
         for h in range(2):
-            send_b[u, h] = done[:, h * LANES : (h + 1) * LANES]
+            send_b[u, h, base : base + height, :] = done[:, h * LANES : (h + 1) * LANES]
 
     def ring_copy(u):
         return pltpu.make_async_remote_copy(
@@ -255,13 +257,29 @@
             device_id_type=MESH,
         )
 
+    def ring_early(u, base):
+        span = pl.ds(base, pair)
+        return pltpu.make_async_remote_copy(
+            src_ref=send_b.at[u, :, span, :],
+            dst_ref=recv_b.at[u, :, span, :],
+            send_sem=ring_send,
+            recv_sem=ring_recv.at[u, 0],
+            device_id=other(0, 1 - 2 * u),
+            device_id_type=MESH,
+        )
+
     for copy in basis_loads[0]:
         copy.wait()
-    compute(jnp.int32(0))
+    compute(0, 0, pair)
     pl.semaphore_wait(barrier, len(sideways) + n_pos - 1)
-    ring_copy(0).start()
+    ring_early(0, 0).start()
     for p in range(1, pos_local):
         locate(p)
+        for copy in basis_loads[p]:
+            copy.wait()
+    for u, base in ((1, 0), (0, pair), (1, pair)):
+        compute(u, base, pair)
+        ring_early(u, base).start()
 
     for copy in small_loads:
         copy.wait()
@@ -282,14 +300,8 @@
             device_id_type=MESH,
         )
 
-    @pl.loop(1, messages + 2)
+    @pl.loop(2, messages + 2)
     def _(u):
-        @pl.when(u == 1)
-        def _():
-            for p in range(1, pos_local):
-                for copy in basis_loads[p]:
-                    copy.wait()
-
         compute(u)
 
         @pl.when((u >= 4) & (u < messages))

time: 48 us -> 48.4 us (level)
  Pallas kernels: 47.2 us -> 47.7 us
where the time goes in v5:
time: 48.4 us; the launch traced here: 48.3 us
  Pallas kernels  47.7 us (99%)
  local copies, waits for them, and re-layouts  0.58 us (1%)
    pallas_call x1, Pallas kernels, body(): pl.pallas_call(functools.partial(kernel, n_pos, n_freq), out_shape=jax.Sh...  47.7 us

profile of v5, /device:TPU:1, one launch (start us, length us, event | category | flops | bytes accessed | tf_op | source)
XLA Modules:
  0.0 48.3 jit_solution(1567882791912586148)
XLA Ops:
  0.0 47.7 %shard_map.55 = f32[4,32]{1,0:T(4,128)S(1)} custom-call(s32[32,64]{1,0:T(8,128)} %bitcast.2, f32[1,256]{1,0:T(1,128)} %bitcast.3, f32[2,4,32]{2,1,0:T(4,128)} %conduct_in.1, f32[4,32]{1,0:T(4,128)} %base_in.1, bf16[2,2,2048,256]{3,2,1,0:T(8,128)(2,1)} %basis_ref.1), custom_call_target="tpu_custom_call" | custom-call | tf_op jit(solution)/shard_map/pallas_call | solution.py:541
  47.7 0.6 %copy.7 = f32[4,32]{1,0:T(4,128)} copy(f32[4,32]{1,0:T(4,128)S(1)} %shard_map.55) | data formatting | bytes 1024

commit v6 on v5

--- a/solution.py
+++ b/solution.py
@@ -101,7 +101,11 @@
         tables.append([(digit + move) % size * below for move in range(size)])
     moves = list(itertools.product(*[range(size) for size in sizes]))[1:]
     moves.sort(key=lambda m: -sum(min(d, z - d) for d, z in zip(m, sizes)))
-    return [sum(table[d] for table, d in zip(tables, m)) for m in moves]
+    lines = []
+    for i, size in enumerate(sizes):
+        rest = sum(table[0] for j, table in enumerate(tables) if j != i)
+        lines.append([rest + tables[i][d] for d in range(1, size)])
+    return [sum(table[d] for table, d in zip(tables, m)) for m in moves], lines
 
 
 def kernel(
@@ -139,6 +143,7 @@
     val_recv,
     halo_send,
     halo_recv,
+    rounds,
 ):
     pos = lax.axis_index("pos")
     freq = lax.axis_index("freq")
@@ -162,6 +167,28 @@
         ]
         for p in range(pos_local)
     ]
+    rows_at = {dp: (pos + dp + n_pos) % n_pos if dp else pos for dp in (-1, 0, 1)}
+    cols_at = [(freq + df) % n_freq for df in range(n_freq)]
+
+    def other(dp, df):
+        return (rows_at[dp], cols_at[df % n_freq] if isinstance(df, int) else (freq + df + n_freq) % n_freq)
+
+    barrier = pltpu.get_barrier_semaphore()
+    walks, lines = walks_of(pos, n_pos)
+    greeted = [other(0, 1), other(0, -1)] + [(target, freq) for line in lines for target in line]
+    for peer in greeted:
+        pl.semaphore_signal(barrier, inc=1, device_id=peer, device_id_type=MESH)
+
+    stages = [[other(0, 1), other(0, -1)]] * (n_freq // 2 - 1)
+    stages += [[(target, freq) for target in line] for line in lines[1:]]
+
+    def round_signal(i):
+        for peer in stages[i]:
+            pl.semaphore_signal(rounds.at[i], inc=1, device_id=peer, device_id_type=MESH)
+
+    def round_wait(i):
+        pl.semaphore_wait(rounds.at[i], len(stages[i]))
+
     foot_load, *small_loads = [
         pltpu.make_async_copy(src, dst, in_sem.at[i])
         for i, (src, dst) in enumerate(
@@ -180,25 +207,11 @@
     for copy in small_loads:
         copy.start()
 
-    rows_at = {dp: (pos + dp + n_pos) % n_pos if dp else pos for dp in (-1, 0, 1)}
-    cols_at = [(freq + df) % n_freq for df in range(n_freq)]
-
-    def other(dp, df):
-        return (rows_at[dp], cols_at[df % n_freq] if isinstance(df, int) else (freq + df + n_freq) % n_freq)
-
     def wait_all(ref, sem):
         pltpu.make_async_copy(ref, ref, sem).wait()
 
-    barrier = pltpu.get_barrier_semaphore()
     near = [(dp, df) for dp in (-1, 0, 1) for df in range(n_freq) if (dp, df) != (0, 0)]
     near.sort(key=lambda d: -min(d[1], n_freq - d[1]) - abs(d[0]) * 0.5)
-    sideways = [(dp, df) for dp, df in near if df != 0]
-    for dp, df in sideways:
-        pl.semaphore_signal(barrier, inc=1, device_id=other(dp, df), device_id_type=MESH)
-
-    walks = walks_of(pos, n_pos)
-    for target in walks:
-        pl.semaphore_signal(barrier, inc=1, device_id=(target, freq), device_id_type=MESH)
 
     expand = iota(i32, (rows, foot), 0) % foot == iota(i32, (rows, foot), 1)
     expand = jnp.where(expand, 1.0, 0.0).astype(bf16)
@@ -271,7 +284,7 @@
     for copy in basis_loads[0]:
         copy.wait()
     compute(0, 0, pair)
-    pl.semaphore_wait(barrier, len(sideways) + n_pos - 1)
+    pl.semaphore_wait(barrier, len(greeted))
     ring_early(0, 0).start()
     for p in range(1, pos_local):
         locate(p)
@@ -324,8 +337,17 @@
                 ring_part(u - 2, c).start()
                 ring_part(u, c).start()
 
-        @pl.when(u == 5)
+        for i in range(len(stages)):
+
+            @pl.when(u == 4 + i)
+            def _():
+                if i > 0:
+                    round_wait(i - 1)
+                round_signal(i)
+
+        @pl.when(u == 4 + len(stages))
         def _():
+            round_wait(len(stages) - 1)
             for i, (dp, df) in enumerate(halo_peers):
                 halo_copy(i, dp, df).start()
 
@@ -570,6 +592,7 @@
             pltpu.SemaphoreType.DMA,
             pltpu.SemaphoreType.DMA,
             pltpu.SemaphoreType.DMA,
+            pltpu.SemaphoreType.REGULAR((len(digits_of(n_pos)) + n_freq // 2 - 2,)),
         ],
         compiler_params=pltpu.CompilerParams(
             collective_id=0, has_side_effects=True, vmem_limit_bytes=50 * 1024 * 1024

time: 48.4 us -> 45.7 us (0.944)
  Pallas kernels: 47.7 us -> 45 us
    pallas_call x1, Pallas kernels: 47.7 us -> 45 us  [body(): pl.pallas_call(functools.partial(kernel, n_pos, n_freq), out_shape=jax.Sh...]
where the time goes in v6:
time: 45.7 us; the launch traced here: 45.6 us
  Pallas kernels  45 us (98%)
  local copies, waits for them, and re-layouts  0.58 us (1%)
    pallas_call x1, Pallas kernels, body(): pl.pallas_call(functools.partial(kernel, n_pos, n_freq), out_shape=jax.Sh...  45 us

profile of v6, /device:TPU:1, one launch (start us, length us, event | category | flops | bytes accessed | tf_op | source)
XLA Modules:
  0.0 45.6 jit_solution(13190937176804653729)
XLA Ops:
  0.0 45.0 %shard_map.55 = f32[4,32]{1,0:T(4,128)S(1)} custom-call(s32[32,64]{1,0:T(8,128)} %bitcast.2, f32[1,256]{1,0:T(1,128)} %bitcast.3, f32[2,4,32]{2,1,0:T(4,128)} %conduct_in.1, f32[4,32]{1,0:T(4,128)} %base_in.1, bf16[2,2,2048,256]{3,2,1,0:T(8,128)(2,1)} %basis_ref.1), custom_call_target="tpu_custom_call" | custom-call | tf_op jit(solution)/shard_map/pallas_call | solution.py:563
  45.0 0.6 %copy.7 = f32[4,32]{1,0:T(4,128)} copy(f32[4,32]{1,0:T(4,128)S(1)} %shard_map.55) | data formatting | bytes 1024

commit v7 on v6

--- a/solution.py
+++ b/solution.py
@@ -314,7 +314,17 @@
         )
 
     @pl.loop(2, messages + 2)
-    def _(u):
+    def _(v):
+        late = messages - 2
+        u = jnp.where(
+            v < late - 4,
+            v,
+            jnp.where(
+                v == late - 4,
+                messages,
+                jnp.where(v <= late, v - 1, jnp.where(v == late + 1, messages + 1, v - 2)),
+            ),
+        )
         compute(u)
 
         @pl.when((u >= 4) & (u < messages))

time: 45.7 us -> 46.3 us (1.013)
  Pallas kernels: 45 us -> 45.6 us
    pallas_call x1, Pallas kernels: 45 us -> 45.6 us  [body(): pl.pallas_call(functools.partial(kernel, n_pos, n_freq), out_shape=jax.Sh...]
where the time goes in v7:
time: 46.3 us; the launch traced here: 46.2 us
  Pallas kernels  45.6 us (98%)
  local copies, waits for them, and re-layouts  0.58 us (1%)
    pallas_call x1, Pallas kernels, body(): pl.pallas_call(functools.partial(kernel, n_pos, n_freq), out_shape=jax.Sh...  45.6 us

profile of v7, /device:TPU:1, one launch (start us, length us, event | category | flops | bytes accessed | tf_op | source)
XLA Modules:
  0.0 46.2 jit_solution(9843147655461872557)
XLA Ops:
  0.0 45.6 %shard_map.55 = f32[4,32]{1,0:T(4,128)S(1)} custom-call(s32[32,64]{1,0:T(8,128)} %bitcast.2, f32[1,256]{1,0:T(1,128)} %bitcast.3, f32[2,4,32]{2,1,0:T(4,128)} %conduct_in.1, f32[4,32]{1,0:T(4,128)} %base_in.1, bf16[2,2,2048,256]{3,2,1,0:T(8,128)(2,1)} %basis_ref.1), custom_call_target="tpu_custom_call" | custom-call | tf_op jit(solution)/shard_map/pallas_call | solution.py:573
  45.6 0.6 %copy.7 = f32[4,32]{1,0:T(4,128)} copy(f32[4,32]{1,0:T(4,128)S(1)} %shard_map.55) | data formatting | bytes 1024

commit v8 on v6

--- a/solution.py
+++ b/solution.py
@@ -526,10 +526,8 @@
         for col in range(1, n_freq):
             group = jnp.where(sub8 == col, value_r[o * n_freq + col], group)
         groups.append(group)
-    wide = None
-    for piece in split3(jnp.concatenate(groups, axis=0)):
-        part = jnp.dot(piece, spread, preferred_element_type=f32)
-        wide = part if wide is None else wide + part
+    pieces = jnp.concatenate(split3(jnp.concatenate(groups, axis=0)), axis=1)
+    wide = jnp.dot(pieces, jnp.concatenate([spread] * 3, axis=0), preferred_element_type=f32)
     wide = jnp.where(keep, wide, 0.0)
     field = jnp.zeros((16, LANES), f32)
     for o in range(3):

time: 45.7 us -> 45.7 us (level)
  no operation moved by 1% of the time
where the time goes in v8:
time: 45.7 us; the launch traced here: 45.6 us
  Pallas kernels  45 us (98%)
  local copies, waits for them, and re-layouts  0.58 us (1%)
    pallas_call x1, Pallas kernels, body(): pl.pallas_call(functools.partial(kernel, n_pos, n_freq), out_shape=jax.Sh...  45 us

profile of v8, /device:TPU:1, one launch (start us, length us, event | category | flops | bytes accessed | tf_op | source)
XLA Modules:
  0.0 45.6 jit_solution(6581187369849523593)
XLA Ops:
  0.0 45.0 %shard_map.55 = f32[4,32]{1,0:T(4,128)S(1)} custom-call(s32[32,64]{1,0:T(8,128)} %bitcast.2, f32[1,256]{1,0:T(1,128)} %bitcast.3, f32[2,4,32]{2,1,0:T(4,128)} %conduct_in.1, f32[4,32]{1,0:T(4,128)} %base_in.1, bf16[2,2,2048,256]{3,2,1,0:T(8,128)(2,1)} %basis_ref.1), custom_call_target="tpu_custom_call" | custom-call | tf_op jit(solution)/shard_map/pallas_call | solution.py:561
  45.0 0.6 %copy.7 = f32[4,32]{1,0:T(4,128)} copy(f32[4,32]{1,0:T(4,128)S(1)} %shard_map.55) | data formatting | bytes 1024

commit v9 on v6

--- a/solution.py
+++ b/solution.py
@@ -104,7 +104,7 @@
     lines = []
     for i, size in enumerate(sizes):
         rest = sum(table[0] for j, table in enumerate(tables) if j != i)
-        lines.append([rest + tables[i][d] for d in range(1, size)])
+        lines.append([rest + tables[i][d] for d in sorted({1, size - 1})])
     return [sum(table[d] for table, d in zip(tables, m)) for m in moves], lines
 
 
@@ -180,7 +180,9 @@
         pl.semaphore_signal(barrier, inc=1, device_id=peer, device_id_type=MESH)
 
     stages = [[other(0, 1), other(0, -1)]] * (n_freq // 2 - 1)
-    stages += [[(target, freq) for target in line] for line in lines[1:]]
+    for size, line in zip(digits_of(n_pos), lines):
+        again = max(1, size // 2 - 1) if line is lines[0] else max(1, size // 2)
+        stages += [[(target, freq) for target in line]] * again
 
     def round_signal(i):
         for peer in stages[i]:
@@ -592,7 +594,7 @@
             pltpu.SemaphoreType.DMA,
             pltpu.SemaphoreType.DMA,
             pltpu.SemaphoreType.DMA,
-            pltpu.SemaphoreType.REGULAR((len(digits_of(n_pos)) + n_freq // 2 - 2,)),
+            pltpu.SemaphoreType.REGULAR((16,)),
         ],
         compiler_params=pltpu.CompilerParams(
             collective_id=0, has_side_effects=True, vmem_limit_bytes=50 * 1024 * 1024

time: 45.7 us -> 47 us (1.028)
  Pallas kernels: 45 us -> 46.3 us
    pallas_call x1, Pallas kernels: 45 us -> 46.3 us  [body(): pl.pallas_call(functools.partial(kernel, n_pos, n_freq), out_shape=jax.Sh...]
where the time goes in v9:
time: 47 us; the launch traced here: 46.9 us
  Pallas kernels  46.3 us (99%)
  local copies, waits for them, and re-layouts  0.58 us (1%)
    pallas_call x1, Pallas kernels, body(): pl.pallas_call(functools.partial(kernel, n_pos, n_freq), out_shape=jax.Sh...  46.3 us

profile of v9, /device:TPU:1, one launch (start us, length us, event | category | flops | bytes accessed | tf_op | source)
XLA Modules:
  0.0 46.9 jit_solution(9349926247184309458)
XLA Ops:
  0.0 46.3 %shard_map.55 = f32[4,32]{1,0:T(4,128)S(1)} custom-call(s32[32,64]{1,0:T(8,128)} %bitcast.2, f32[1,256]{1,0:T(1,128)} %bitcast.3, f32[2,4,32]{2,1,0:T(4,128)} %conduct_in.1, f32[4,32]{1,0:T(4,128)} %base_in.1, bf16[2,2,2048,256]{3,2,1,0:T(8,128)(2,1)} %basis_ref.1), custom_call_target="tpu_custom_call" | custom-call | tf_op jit(solution)/shard_map/pallas_call | solution.py:565
  46.3 0.6 %copy.7 = f32[4,32]{1,0:T(4,128)} copy(f32[4,32]{1,0:T(4,128)S(1)} %shard_map.55) | data formatting | bytes 1024
